TPU v7x, 32 devices: a whole 2x2x4 slice. The times are simulated.
32 devices in a mesh: dp: 8 (over z, y), head: 4 (over x, core).
Axes of the slice: x: 2, y: 2, z: 4, core: 2. Of those that a mesh axis runs over, the one named last changes fastest.
Arguments:
- tokens: bfloat16 [8, 1024, 768], P('dp', 'head'), may hold values from -6 to 6
- memory: bfloat16 [8, 2048, 768], P('dp', 'head'), may hold values from -6 to 6
- text_length: int32 [8], P('dp'), may hold values from 256 to 1024, as said below
- patch_count: int32 [8], P('dp'), may hold values from 512 to 2048, as said below
- self_gain: bfloat16 [768], P(('dp', 'head')), may hold values from 0.5 to 1.5
- self_query: bfloat16 [768, 768], P(('dp', 'head')), may hold values from -0.21875 to 0.21875
- self_key: bfloat16 [768, 768], P(('dp', 'head')), may hold values from -0.21875 to 0.21875
- self_value: bfloat16 [768, 768], P(('dp', 'head')), may hold values from -0.21875 to 0.21875
- self_out: bfloat16 [768, 768], P(('dp', 'head')), may hold values from -3.5 to 3.5
- cross_gain: bfloat16 [768], P(('dp', 'head')), may hold values from 0.5 to 1.5
- cross_query: bfloat16 [768, 768], P(('dp', 'head')), may hold values from -0.21875 to 0.21875
- cross_key: bfloat16 [768, 768], P(('dp', 'head')), may hold values from -0.21875 to 0.21875
- cross_value: bfloat16 [768, 768], P(('dp', 'head')), may hold values from -0.21875 to 0.21875
- cross_out: bfloat16 [768, 768], P(('dp', 'head')), may hold values from -6 to 6
- mlp_gain: bfloat16 [768], P(('dp', 'head')), may hold values from 0.5 to 1.5
- mlp_gate: bfloat16 [768, 2048], P(('dp', 'head')), may hold values from -0.21875 to 0.21875
- mlp_up: bfloat16 [768, 2048], P(('dp', 'head')), may hold values from -0.21875 to 0.21875
- mlp_down: bfloat16 [2048, 768], P(('dp', 'head')), may hold values from -0.125 to 0.125
- output_grad: bfloat16 [8, 1024, 768], P('dp', 'head'), may hold values from -6 to 6
Outputs:
- output: bfloat16 [8, 1024, 768], P('dp', 'head')
- input_grad: float32 [8, 1024, 768], P('dp', 'head')
- memory_grad: float32 [8, 2048, 768], P('dp', 'head')
- self_dgain: float32 [768], P(('dp', 'head'))
- self_dquery: float32 [768, 768], P(('dp', 'head'))
- self_dkey: float32 [768, 768], P(('dp', 'head'))
- self_dvalue: float32 [768, 768], P(('dp', 'head'))
- self_dout: float32 [768, 768], P(('dp', 'head'))
- cross_dgain: float32 [768], P(('dp', 'head'))
- cross_dquery: float32 [768, 768], P(('dp', 'head'))
- cross_dkey: float32 [768, 768], P(('dp', 'head'))
- cross_dvalue: float32 [768, 768], P(('dp', 'head'))
- cross_dout: float32 [768, 768], P(('dp', 'head'))
- mlp_dgain: float32 [768], P(('dp', 'head'))
- mlp_dgate: float32 [768, 2048], P(('dp', 'head'))
- mlp_dup: float32 [768, 2048], P(('dp', 'head'))
- mlp_ddown: float32 [2048, 768], P(('dp', 'head'))
Inputs may be any that keep to these rules, and one draw needn't show every extreme that they name: `text_length`: positions at or past a chart's length are padding; some chart uses all 1024 positions and some only 256. `patch_count`: the valid patches are the first ones of a chart's grid; some chart fills all 2048 and some only 512.
All inputs are finite; a program needn't handle non-finite values.
Results may differ from a plain program's by a relative error of at most 0.02.
Values may be sent and summed in bfloat16 or wider, within the bound.
No kernel may reach another device: no remote copies, remote signals or barrier semaphores. Data moves between devices by JAX's collectives and lax.ppermute only.
A program may use at most 192 MiB of HBM per device.

v0:
```python
import functools
import math

import jax
import jax.numpy as jnp
from jax import lax
from jax.experimental import pallas as pl
from jax.experimental.pallas import tpu as pltpu
from jax.sharding import Mesh
from jax.sharding import PartitionSpec as P

HEAD_DIM = 64
PAIR_LANES = 128
NEG_FILL = -1e30
EPS = 1e-06
F32 = jnp.float32
LOW = jnp.bfloat16


NT = (((1,), (1,)), ((), ()))
TN = (((0,), (0,)), ((), ()))


def dot_nt(left, right):
    return lax.dot_general(left, right, NT, preferred_element_type=F32)


def dot_tn(left, right):
    return lax.dot_general(left, right, TN, preferred_element_type=F32)


def dot_nn(left, right):
    return jnp.dot(left, right, preferred_element_type=F32)


FIXED = 3
SPANS = 4


def query_limits(info, queries, causal):
    last = info[0] - 1
    if not causal:
        return jnp.full((1, queries), last, jnp.int32), last
    lanes = lax.broadcasted_iota(jnp.int32, (1, queries), 1)
    span = queries // 2
    swapped = jnp.where(lanes < span, lanes + info[2] * span, lanes - info[2] * span)
    return jnp.minimum(info[1] + swapped, last), jnp.minimum(info[1] + queries - 1, last)


def key_places(info, chunk, span, queries, j):
    parts = chunk // span
    starts = [info[FIXED + j * parts + i] for i in range(parts)]
    inner = lax.broadcasted_iota(jnp.int32, (span, queries), 0)
    first = functools.reduce(jnp.minimum, starts)
    return jnp.concatenate([start + inner for start in starts], axis=0), first


def first_place(info, chunk, span, j):
    parts = chunk // span
    return functools.reduce(jnp.minimum, [info[FIXED + j * parts + i] for i in range(parts)])


def head_lanes(head):
    lanes = lax.broadcasted_iota(jnp.int32, (1, PAIR_LANES), 1)
    return (lanes // HEAD_DIM) == head


def fold(values, op):
    rows, columns = values.shape
    return op(values.reshape(rows // 8, 8, columns), axis=0)


def forward_kernel(causal, chunk, span, info, q_ref, k_ref, v_ref, c_ref, lse_ref, s_ref, m_ref, l_ref, a_ref):
    queries = q_ref.shape[0]
    chunks = k_ref.shape[0] // chunk
    scaling = 1.0 / math.sqrt(HEAD_DIM)
    limit, latest = query_limits(info, queries, causal)
    q_all = q_ref[...] * jnp.asarray(scaling, q_ref.dtype)
    q_heads = [jnp.where(head_lanes(h), q_all, jnp.zeros_like(q_all)) for h in range(2)]
    m_ref[...] = jnp.full(m_ref.shape, NEG_FILL, F32)
    l_ref[...] = jnp.zeros(l_ref.shape, F32)
    a_ref[...] = jnp.zeros(a_ref.shape, F32)

    @pl.loop(0, chunks)
    def _(j):
        @pl.when(first_place(info, chunk, span, j) <= latest)
        def _():
            rows = pl.ds(pl.multiple_of(j * chunk, chunk), chunk)
            keys = k_ref[rows, :]
            place, _ = key_places(info, chunk, span, queries, j)
            allowed = place <= limit
            for h in range(2):
                scores = jnp.where(allowed, dot_nt(keys, q_heads[h]), NEG_FILL)
                s_ref[h, rows, :] = scores
                m_ref[h] = jnp.maximum(m_ref[h], fold(scores, jnp.max))

    highest = [jnp.max(m_ref[h], axis=0, keepdims=True) for h in range(2)]

    @pl.loop(0, chunks)
    def _(j):
        @pl.when(first_place(info, chunk, span, j) <= latest)
        def _():
            rows = pl.ds(pl.multiple_of(j * chunk, chunk), chunk)
            values = v_ref[rows, :]
            for h in range(2):
                weight = jnp.exp(s_ref[h, rows, :] - highest[h])
                l_ref[h] = l_ref[h] + fold(weight, jnp.sum)
                a_ref[h] = a_ref[h] + dot_tn(values, weight.astype(LOW))

    parts = []
    for h in range(2):
        total = jnp.sum(l_ref[h], axis=0, keepdims=True)
        lse_ref[0, pl.ds(h, 1), :] = highest[h] + jnp.log(total)
        parts.append(a_ref[h, pl.ds(h * HEAD_DIM, HEAD_DIM), :] / total)
    c_ref[...] = jnp.concatenate(parts, axis=0).T.astype(c_ref.dtype)


def backward_kernel(causal, chunk, span, info, q_ref, k_ref, v_ref, c_ref, g_ref, lse_ref, dq_ref, dk_ref, dv_ref, a_ref):
    queries = q_ref.shape[0]
    chunks = k_ref.shape[0] // chunk
    scaling = 1.0 / math.sqrt(HEAD_DIM)
    limit, latest = query_limits(info, queries, causal)
    q_all = q_ref[...] * jnp.asarray(scaling, q_ref.dtype)
    g_all = g_ref[...]
    q_heads = [jnp.where(head_lanes(h), q_all, jnp.zeros_like(q_all)) for h in range(2)]
    g_heads = [jnp.where(head_lanes(h), g_all, jnp.zeros_like(g_all)) for h in range(2)]
    product = (c_ref[...].astype(F32) * g_all.astype(F32)).T
    centres = [
        jnp.sum(product[h * HEAD_DIM : (h + 1) * HEAD_DIM], axis=0, keepdims=True) for h in range(2)
    ]
    logs = [lse_ref[0, pl.ds(h, 1), :] for h in range(2)]
    a_ref[...] = jnp.zeros(a_ref.shape, F32)

    @pl.loop(0, chunks)
    def _(j):
        start = first_place(info, chunk, span, j)
        rows = pl.ds(pl.multiple_of(j * chunk, chunk), chunk)

        @pl.when(start <= latest)
        def _():
            keys = k_ref[rows, :]
            values = v_ref[rows, :]
            place, _ = key_places(info, chunk, span, queries, j)
            allowed = place <= limit
            dk = jnp.zeros((chunk, PAIR_LANES), F32)
            dv = jnp.zeros((chunk, PAIR_LANES), F32)
            for h in range(2):
                scores = jnp.where(allowed, dot_nt(keys, q_heads[h]), NEG_FILL)
                prob = jnp.exp(scores - logs[h])
                dprob = dot_nt(values, g_heads[h])
                dv = dv + dot_nn(prob.astype(LOW), g_heads[h])
                dscore = (prob * (dprob - centres[h])).astype(LOW)
                dk = dk + dot_nn(dscore, q_heads[h])
                a_ref[h] = a_ref[h] + dot_tn(keys, dscore)
            dk_ref[rows, :] = dk.astype(dk_ref.dtype)
            dv_ref[rows, :] = dv.astype(dv_ref.dtype)

        @pl.when(start > latest)
        def _():
            dk_ref[rows, :] = jnp.zeros((chunk, PAIR_LANES), dk_ref.dtype)
            dv_ref[rows, :] = jnp.zeros((chunk, PAIR_LANES), dv_ref.dtype)

    parts = [a_ref[h, pl.ds(h * HEAD_DIM, HEAD_DIM), :] for h in range(2)]
    dq_ref[...] = (jnp.concatenate(parts, axis=0).T * scaling).astype(dq_ref.dtype)


def lane_spec(rows):
    return pl.BlockSpec((rows, PAIR_LANES), lambda i, info: (0, i))


def stat_spec(queries):
    return pl.BlockSpec((1, 2, queries), lambda i, info: (i, 0, 0))


def attention_forward(info, queries, keys, values, causal, span):
    chunk = math.gcd(SPANS * span, keys.shape[0])
    rows, features = queries.shape
    key_rows = keys.shape[0]
    pairs = features // PAIR_LANES
    return pl.pallas_call(
        functools.partial(forward_kernel, causal, chunk, span),
        out_shape=(
            jax.ShapeDtypeStruct((rows, features), LOW),
            jax.ShapeDtypeStruct((pairs, 2, rows), F32),
        ),
        grid_spec=pltpu.PrefetchScalarGridSpec(
            num_scalar_prefetch=1,
            grid=(pairs,),
            in_specs=[lane_spec(rows), lane_spec(key_rows), lane_spec(key_rows)],
            out_specs=[lane_spec(rows), stat_spec(rows)],
            scratch_shapes=[
                pltpu.VMEM((2, key_rows, rows), F32),
                pltpu.VMEM((2, 8, rows), F32),
                pltpu.VMEM((2, 8, rows), F32),
                pltpu.VMEM((2, PAIR_LANES, rows), F32),
            ],
        ),
        compiler_params=pltpu.CompilerParams(vmem_limit_bytes=VMEM_LIMIT),
        cost_estimate=pl.CostEstimate(flops=rows, transcendentals=0, bytes_accessed=0),
    )(info, queries, keys, values)


def attention_backward(info, queries, keys, values, context, grads, lse, causal, span):
    chunk = math.gcd(SPANS * span, keys.shape[0])
    rows, features = queries.shape
    key_rows = keys.shape[0]
    pairs = features // PAIR_LANES
    return pl.pallas_call(
        functools.partial(backward_kernel, causal, chunk, span),
        out_shape=(
            jax.ShapeDtypeStruct((rows, features), LOW),
            jax.ShapeDtypeStruct((key_rows, features), LOW),
            jax.ShapeDtypeStruct((key_rows, features), LOW),
        ),
        grid_spec=pltpu.PrefetchScalarGridSpec(
            num_scalar_prefetch=1,
            grid=(pairs,),
            in_specs=[
                lane_spec(rows),
                lane_spec(key_rows),
                lane_spec(key_rows),
                lane_spec(rows),
                lane_spec(rows),
                stat_spec(rows),
            ],
            out_specs=[lane_spec(rows), lane_spec(key_rows), lane_spec(key_rows)],
            scratch_shapes=[pltpu.VMEM((2, PAIR_LANES, rows), F32)],
        ),
        compiler_params=pltpu.CompilerParams(vmem_limit_bytes=VMEM_LIMIT),
        cost_estimate=pl.CostEstimate(flops=rows, transcendentals=0, bytes_accessed=0),
    )(info, queries, keys, values, context, grads, lse)


SMEM_SPEC = pl.BlockSpec(memory_space=pltpu.SMEM)


def vmem_specs(number):
    return [pl.BlockSpec(memory_space=pltpu.VMEM)] * number


def cuts_of(widths):
    return [sum(widths[:i]) for i in range(len(widths))]


def place_blocks(index, first, later, targets):
    half, rows, _ = first.shape
    cuts = cuts_of([target.shape[1] for target in targets])

    @pl.loop(0, 2 * half)
    def _(step):
        at = index[step]
        place = pl.ds(pl.multiple_of(step * rows, rows), rows)

        def put(source, block):
            for cut, target in zip(cuts, targets):
                target[place, :] = source[block, :, pl.ds(cut, target.shape[1])]

        @pl.when(at < half)
        def _():
            put(first, at)

        @pl.when(at >= half)
        def _():
            put(later, at - half)


def send_order(index, whole, keep, give):
    half, rows, _ = keep.shape

    @pl.loop(0, half)
    def _(step):
        for side, target in enumerate((keep, give)):
            at = pl.ds(pl.multiple_of(index[step + side * half] * rows, rows), rows)
            target[step] = whole[at, :]


def whole_kernel(index, first, later, *targets):
    place_blocks(index, first, later, targets)


def to_whole(first, later, index, widths):
    half, rows, columns = first.shape
    count = 2 * half
    if rows % 16:
        blocks = jnp.concatenate([first, later], axis=0)
        whole = jnp.take(blocks, index, axis=0).reshape(count * rows, columns)
        return [whole[:, cut : cut + width] for cut, width in zip(cuts_of(widths), widths)]
    return run_kernel(
        whole_kernel,
        [low_shape(count * rows, width) for width in widths],
        count * rows * columns,
        [index],
        [first, later],
    )


def staged_kernel(body, late, sizes, *refs):
    parts, at = [], 0
    for size in sizes:
        parts.append(refs[at : at + size])
        at += size
    tables, arrays, streamed, outs, scratch, held_in, held_out, (in_sems, out_sems) = parts
    loads = [
        pltpu.make_async_copy(a, b, in_sems.at[i]) for i, (a, b) in enumerate(zip(arrays, held_in))
    ]
    for load in loads:
        load.start()

    def ready():
        for load in loads:
            load.wait()

    if late:
        body(ready, *tables, *held_in, *streamed, *held_out, *scratch)
    else:
        ready()
        body(*tables, *held_in, *streamed, *held_out, *scratch)
    stores = [
        pltpu.make_async_copy(a, b, out_sems.at[i]) for i, (a, b) in enumerate(zip(held_out, outs))
    ]
    for store in stores:
        store.start()
    for store in stores:
        store.wait()


HBM_SPEC = pl.BlockSpec(memory_space=pltpu.HBM)


def run_kernel(body, out_shape, cost, tables, arrays, scratch=(), streamed=(), late=False):
    sizes = (len(tables), len(arrays), len(streamed), len(out_shape), len(scratch))
    sizes += (len(arrays), len(out_shape), 2)
    held = [pltpu.VMEM(x.shape, x.dtype) for x in [*arrays, *out_shape]]
    sems = [pltpu.SemaphoreType.DMA((len(arrays),)), pltpu.SemaphoreType.DMA((len(out_shape),))]
    return pl.pallas_call(
        functools.partial(staged_kernel, body, late, sizes),
        out_shape=out_shape,
        in_specs=[SMEM_SPEC] * len(tables) + [HBM_SPEC] * (len(arrays) + len(streamed)),
        out_specs=[HBM_SPEC] * len(out_shape),
        scratch_shapes=list(scratch) + held + sems,
        compiler_params=pltpu.CompilerParams(vmem_limit_bytes=VMEM_LIMIT),
        cost_estimate=pl.CostEstimate(flops=cost // 1000, transcendentals=0, bytes_accessed=0),
    )(*tables, *arrays, *streamed)


VMEM_LIMIT = 56 << 20


def low_shape(*shape):
    return jax.ShapeDtypeStruct(shape, LOW)


def full_shape(*shape):
    return jax.ShapeDtypeStruct(shape, F32)


def unit_tile(source, at, second):
    lanes = 2 * HEAD_DIM
    start = 2 * at * lanes + (HEAD_DIM if second else 0)
    return jnp.concatenate(
        [source[:, pl.ds(start, HEAD_DIM)], source[:, pl.ds(start + lanes, HEAD_DIM)]], axis=1
    )


def shards_kernel(kinds, place, *refs):
    sources, targets = refs[:-2], refs[-2:]

    def write(target, second):
        cut = 0
        for kind, source in zip(kinds, sources):
            columns = source.shape[1]
            if kind == "all":
                target[:, pl.ds(cut, columns)] = source[...]
                cut += columns
                continue
            if kind == "half":
                start = columns // 2 if second else 0
                target[:, pl.ds(cut, columns // 2)] = source[:, pl.ds(start, columns // 2)]
            else:
                for tile in range(columns // 256):
                    target[:, pl.ds(cut + 128 * tile, 128)] = unit_tile(source, tile, second)
            cut += columns // 2

    @pl.when(place[0] == 0)
    def _():
        write(targets[0], False)
        write(targets[1], True)

    @pl.when(place[0] != 0)
    def _():
        write(targets[0], True)
        write(targets[1], False)


def rows_kernel(widths, piece, place, mine, other, down, *targets):
    *widths, matrices, extra = widths
    rows = mine.shape[0]

    def write(upper, lower):
        cut = 0
        for target, width in zip(targets[:-1], widths):
            target[0, pl.ds(0, rows), :] = upper[:, pl.ds(cut, width)]
            target[0, pl.ds(rows, rows), :] = lower[:, pl.ds(cut, width)]
            cut += width
        packed = targets[-1]
        columns = (mine.shape[1] - cut - extra) // matrices
        step = 8
        base = matrices * (2 * rows // piece) * columns
        last = base + down.shape[1] * (down.shape[0] // piece)
        for start in range(0, 2 * rows, step):
            source = upper if start < rows else lower
            number, inner = start // piece, start % piece
            for matrix in range(matrices):
                place_at = (matrix * (2 * rows // piece) + number) * columns
                packed[pl.ds(inner, step), pl.ds(place_at, columns)] = source[
                    pl.ds(start % rows, step), pl.ds(cut + matrix * columns, columns)
                ]
            packed[pl.ds(inner, step), pl.ds(last + number * extra, extra)] = source[
                pl.ds(start % rows, step), pl.ds(cut + matrices * columns, extra)
            ]
        width = down.shape[1]
        for number in range(down.shape[0] // piece):
            packed[:, pl.ds(base + number * width, width)] = down[pl.ds(number * piece, piece), :]

    @pl.when(place[0] == 0)
    def _():
        write(mine, other)

    @pl.when(place[0] != 0)
    def _():
        write(other, mine)


def cut_shards(place, shards, kinds):
    rows = shards[0].shape[0]
    columns = sum(w.shape[1] if k == "all" else w.shape[1] // 2 for w, k in zip(shards, kinds))
    return run_kernel(
        functools.partial(shards_kernel, kinds), [low_shape(rows, columns)] * 2, rows * columns, [place], shards
    )


def join_rows(place, mine, other, down, widths, extra, piece):
    rows = 2 * mine.shape[0]
    rest = mine.shape[1] - sum(widths)
    packed = rest * (rows // piece) + down.shape[1] * (down.shape[0] // piece)
    return run_kernel(
        functools.partial(rows_kernel, [*widths, 2, extra], piece),
        [low_shape(1, rows, width) for width in widths] + [low_shape(piece, packed)],
        rows * rest,
        [place],
        [mine, other, down],
    )


def pieces_kernel(cut, source, target, held, sem):
    blocks, pieces, piece, columns = held.shape
    copies = [
        pltpu.make_async_copy(
            source.at[:, :, pl.ds(cut + i * columns, columns)], held.at[:, i], sem.at[i]
        )
        for i in range(pieces)
    ]
    for copy in copies:
        copy.start()
    for copy in copies:
        copy.wait()
    target[...] = held[...].reshape(target.shape)


def from_pieces(packed, cut, pieces, columns):
    blocks, piece, _ = packed.shape
    return pl.pallas_call(
        functools.partial(pieces_kernel, cut),
        out_shape=low_shape(blocks * pieces * piece, columns),
        in_specs=[HBM_SPEC],
        out_specs=pl.BlockSpec(memory_space=pltpu.VMEM),
        scratch_shapes=[
            pltpu.VMEM((blocks, pieces, piece, columns), LOW),
            pltpu.SemaphoreType.DMA((pieces,)),
        ],
        cost_estimate=pl.CostEstimate(flops=1000, transcendentals=0, bytes_accessed=0),
    )(packed)


def normalize(values):
    inverse = lax.rsqrt(jnp.mean(values * values, axis=-1, keepdims=True) + EPS)
    return values * inverse, inverse


def norm_back(normed, inverse, gain, grads):
    scaled = grads * gain
    return inverse * (scaled - normed * jnp.mean(scaled * normed, axis=-1, keepdims=True))


def gelu_parts(gate):
    factor = math.sqrt(2.0 / math.pi)
    inner = jnp.tanh(factor * (gate + 0.044715 * gate * gate * gate))
    value = 0.5 * gate * (1.0 + inner)
    slope = 0.5 * (1.0 + inner) + 0.5 * gate * (1.0 - inner * inner) * factor * (
        1.0 + 3.0 * 0.044715 * gate * gate
    )
    return value, slope


def head_slices(place, half):
    mine = pl.ds(pl.multiple_of(place[0] * half, half), half)
    other = pl.ds(pl.multiple_of((1 - place[0]) * half, half), half)
    return mine, other


def project_heads(gain_cols, token_m, token_g, weights, rows_ref, normed_ref, heads):
    gain_rows = gain_cols.astype(F32).T[0:8]
    rows_ref[...] = gain_rows
    groups, own, _ = token_m.shape
    for group in range(groups):
        for side, source in enumerate((token_m, token_g)):
            plain, _ = normalize(source[group].astype(F32))
            at = pl.ds((2 * group + side) * own, own)
            normed_ref[at, :] = (plain * gain_rows[0:1]).astype(LOW)
    for number, (weight, target) in enumerate(zip(weights, heads)):
        target[...] = dot_nn(normed_ref[pl.ds(0, target.shape[0]), :], weight[...]).astype(LOW)


def query_kernel(packed, *refs):
    if packed:
        index_a, index_b, first_a, later_a, first_b, later_b, token_m, token_g = refs[:8]
        rows_ref, normed_ref, q_ref, k_ref, v_ref, wq, gain_cols, wk, wv = refs[8:]
        place_blocks(index_a, first_a, later_a, [wq, gain_cols])
        place_blocks(index_b, first_b, later_b, [wk, wv])
    else:
        wq, gain_cols, wk, wv, token_m, token_g = refs[:6]
        rows_ref, normed_ref, q_ref, k_ref, v_ref = refs[6:]
    heads = (q_ref, k_ref, v_ref)
    project_heads(gain_cols[...], token_m, token_g, (wq, wk, wv), rows_ref, normed_ref, heads)


def add_context(place, target, base, c_m, c_g, w_m, w_g):
    rows, half = c_m.shape
    own = rows // 2
    mine, other = head_slices(place, half)
    for side in range(2):
        at = pl.ds(side * own, own)
        left = c_m[at, :]
        right = c_g[pl.ds((1 - side) * own, own), :]
        for weight, columns in ((w_m, mine), (w_g, other)):
            value = dot_nn(left, weight[mine, :]) + dot_nn(right, weight[other, :])
            target[at, columns] = base(side, columns) + value


def cross_query_kernel(place, token_m, token_g, c_m, c_g, w_m, w_g, rows_ref, wq, h_ref, normed_ref, q_ref):
    tokens = (token_m, token_g)
    base = lambda side, columns: tokens[side][:, columns].astype(F32)
    add_context(place, h_ref, base, c_m, c_g, w_m, w_g)
    plain, _ = normalize(h_ref[...])
    normed_ref[...] = (plain * rows_ref[1:2, :]).astype(LOW)
    q_ref[...] = dot_nn(normed_ref[...], wq[...]).astype(LOW)


def memory_kernel(packed, *refs):
    if packed:
        index, first, later, patch_m, patch_g, k_ref, v_ref, wk, wv = refs
        place_blocks(index, first, later, [wk, wv])
    else:
        wk, wv, patch_m, patch_g, k_ref, v_ref = refs
    count = patch_m.shape[0]
    step = math.gcd(count, 512)
    for side, source in enumerate((patch_m, patch_g)):

        @pl.loop(0, count // step)
        def _(number):
            part = source[pl.ds(pl.multiple_of(number * step, step), step), :]
            place = pl.ds(pl.multiple_of(side * count + number * step, step), step)
            k_ref[place, :] = dot_nn(part, wk[...]).astype(LOW)
            v_ref[place, :] = dot_nn(part, wv[...]).astype(LOW)


def lane_column(column, lane):
    lanes = lax.broadcasted_iota(jnp.int32, (1, PAIR_LANES), 1)
    return jnp.where(lanes == lane, column, 0.0)


def mlp_kernel(
    chunk,
    ready,
    place,
    h_in,
    c_m,
    c_g,
    out_m,
    out_g,
    rows_ref,
    cols_ref,
    g_m,
    g_g,
    w_ref,
    h_ref,
    part_ref,
    keep_ref,
    give_ref,
    gain_ref,
    grad_ref,
    gate_w,
    up_w,
    down_w,
    a_ref,
    t_ref,
    g_ref,
    p_acc,
    d_acc,
    r_acc,
    sems,
):
    blocks, pieces, piece, units = gate_w.shape
    down_pieces, width = down_w.shape[1], down_w.shape[3]
    total = blocks * pieces * piece
    own = g_m.shape[0]
    moves = []
    for number in range(pieces):
        moves.append((w_ref.at[:, :, pl.ds(number * units, units)], gate_w.at[:, number]))
    for number in range(pieces):
        moves.append((w_ref.at[:, :, pl.ds((pieces + number) * units, units)], up_w.at[:, number]))
    base = 2 * pieces * units
    for number in range(down_pieces):
        moves.append((w_ref.at[:, :, pl.ds(base + number * width, width)], down_w.at[:, number]))
    copies = [pltpu.make_async_copy(a, b, sems.at[i]) for i, (a, b) in enumerate(moves)]
    for copy in copies:
        copy.start()
    ready()
    add_context(
        place, h_ref, lambda side, columns: h_in[pl.ds(side * own, own), columns], c_m, c_g, out_m, out_g
    )
    plain, _ = normalize(h_ref[...])
    a_ref[...] = (plain * rows_ref[2:3, :]).astype(LOW)
    t_ref[...] = a_ref[...].T
    g_ref[pl.ds(0, own), :] = g_m[...]
    g_ref[pl.ds(own, own), :] = g_g[...]
    p_acc[...] = jnp.zeros(p_acc.shape, F32)
    d_acc[...] = jnp.zeros(d_acc.shape, F32)
    r_acc[...] = jnp.zeros(r_acc.shape, F32)
    for copy in copies:
        copy.wait()

    per_block = down_pieces * piece
    step_blocks = chunk // per_block

    @pl.loop(0, units // chunk)
    def _(step):
        start = pl.multiple_of(step * chunk, chunk)
        a_in = a_ref[...]
        g_in = g_ref[...]
        columns = pl.ds(start, chunk)
        gate_part = gate_w[:, :, :, columns].reshape(total, chunk)
        up_part = up_w[:, :, :, columns].reshape(total, chunk)
        down_at = pl.ds(step * step_blocks, step_blocks)
        down_part = down_w[down_at].reshape(chunk, width)
        gate = dot_nn(a_in, gate_part)
        up = dot_nn(a_in, up_part)
        active, slope = gelu_parts(gate)
        mixed = (active * up).astype(LOW)
        grad = dot_nt(g_in, down_part)
        gate_low = (grad * up * slope).astype(LOW)
        up_low = (grad * active).astype(LOW)
        d_acc[...] += dot_nn(mixed, down_part)
        p_acc[...] += dot_nt(gate_low, gate_part) + dot_nt(up_low, up_part)
        dgate = dot_nn(t_ref[...], gate_low)
        dup = dot_nn(t_ref[...], up_low)
        gain_terms = dgate * gate_part.astype(F32) + dup * up_part.astype(F32)
        for lane in range(0, chunk, PAIR_LANES):
            r_acc[...] += gain_terms[:, lane : lane + PAIR_LANES]
        dgate = dgate.astype(LOW).reshape(blocks, pieces, piece, chunk)
        dup = dup.astype(LOW).reshape(blocks, pieces, piece, chunk)
        for number in range(pieces):
            gate_at = pl.multiple_of(number * units + start, chunk)
            up_at = pl.multiple_of((pieces + number) * units + start, chunk)
            grad_ref[:, :, pl.ds(gate_at, chunk)] = dgate[:, number]
            grad_ref[:, :, pl.ds(up_at, chunk)] = dup[:, number]
        ddown = dot_tn(mixed, g_in).astype(LOW).reshape(step_blocks, down_pieces, piece, width)
        for number in range(down_pieces):
            grad_ref[down_at, :, pl.ds(base + number * width, width)] = ddown[:, number]

    part_ref[...] = p_acc[...].astype(LOW)
    keep_ref[...] = d_acc[pl.ds(0, own), :]
    give_ref[...] = d_acc[pl.ds(own, own), :].astype(LOW)
    summed = jnp.sum(r_acc[...], axis=1, keepdims=True)
    gain_ref[...] = lane_column(summed / cols_ref[:, 2:3].astype(F32), 2)


def branch_kernel(gain_at, place, *refs):
    h_ref, rows_ref, part_m, part_g, w_m, w_g = refs[:6]
    base, (d_ref, low_ref, c_ref) = refs[6:-3], refs[-3:]
    rows = h_ref.shape[0]
    own = rows // 2
    half = w_m.shape[1]
    mine, other = head_slices(place, half)
    for side in range(2):
        at = pl.ds(side * own, own)
        plain, inverse = normalize(h_ref[at, :])
        got = part_g[pl.ds((1 - side) * own, own), :]
        grads = part_m[at, :].astype(F32) + got.astype(F32)
        value = norm_back(plain, inverse, rows_ref[gain_at : gain_at + 1, :], grads)
        before = base[side][...].astype(F32) if len(base) == 2 else base[0][at, :]
        d_ref[at, :] = before + value
    low_ref[...] = d_ref[...].astype(LOW)
    value = dot_nt(low_ref[:, mine], w_m[mine, :]) + dot_nt(low_ref[:, other], w_g[mine, :])
    c_ref[...] = value.astype(LOW)


def dot_rows(left, right):
    columns = left.shape[1]
    step = math.gcd(columns, 256)
    return [(i, dot_tn(left[:, i : i + step], right)) for i in range(0, columns, step)]


def out_grad(place, whole, cut, c_m, c_g, branch):
    rows, half = c_m.shape
    own = rows // 2
    mine, other = head_slices(place, half)
    grads = branch[:, mine]
    columns = pl.ds(cut, half)
    whole[mine, columns] = dot_tn(c_m[...], grads).astype(LOW)
    value = dot_tn(c_g[pl.ds(own, own), :], grads[:own]) + dot_tn(c_g[pl.ds(0, own), :], grads[own:])
    whole[other, columns] = value.astype(LOW)


def weight_grads(targets, lefts, rights, gain_acc=None):
    features = lefts[0].shape[1]
    step = math.gcd(features, 256)

    for number in range(features // step):
        at = pl.ds(number * step, step)
        turned = [left[:, at].T for left in lefts]
        for (whole, cut, weight), terms in zip(targets, rights):
            width = terms[0].shape[1]
            value = sum(dot_nn(left, right[...]) for left, right in zip(turned, terms))
            whole[at, pl.ds(cut, width)] = value.astype(LOW)
            if weight is not None:
                products = value * weight[at, :].astype(F32)
                gain_acc[at, :] += sum(
                    products[:, lane : lane + PAIR_LANES] for lane in range(0, width, PAIR_LANES)
                )


def finish_blocks(packed, refs, whole_a, whole_b):
    if packed:
        index_a, index_b, keep_a, give_a, keep_b, give_b = refs
        send_order(index_a, whole_a, keep_a, give_a)
        send_order(index_b, whole_b, keep_b, give_b)


def cross_grads_kernel(packed, place, *refs):
    index, refs = (refs[:2], refs[2:]) if packed else ((), refs)
    c_m, c_g, branch, normed, dq, patch_m, patch_g, dk, dv, wq, cols_ref = refs[:11]
    gain_ref, *outs, whole_a, whole_b, gain_acc = refs[11:]
    half = dq.shape[1]
    count = patch_m.shape[0]
    gain_acc[...] = jnp.zeros(gain_acc.shape, F32)
    out_grad(place, whole_a, 0, c_m, c_g, branch)
    weight_grads([(whole_a, half, wq)], [normed], [[dq]], gain_acc)
    halves = [[g.at[pl.ds(i * count, count), :] for i in range(2)] for g in (dk, dv)]
    weight_grads(
        [(whole_b, 0, None), (whole_b, half, None)], [patch_m, patch_g], halves
    )
    summed = jnp.sum(gain_acc[...], axis=1, keepdims=True)
    gain_ref[...] = lane_column(summed / cols_ref[:, 1:2].astype(F32), 1)
    finish_blocks(packed, (*index, *outs), whole_a, whole_b)


def self_grads_kernel(packed, place, *refs):
    index, refs = (refs[:2], refs[2:]) if packed else ((), refs)
    c_m, c_g, branch, normed, dq, dk, dv, wq, wk, wv, cols_ref, gain_two, gain_three = refs[:13]
    *outs, whole_a, whole_b, gain_acc = refs[13:]
    rows, half = dq.shape
    gain_acc[...] = jnp.zeros(gain_acc.shape, F32)
    weight_grads([(whole_a, 0, wq)], [normed.at[pl.ds(0, rows), :]], [[dq]], gain_acc)
    out_grad(place, whole_a, half, c_m, c_g, branch)
    weight_grads(
        [(whole_b, 0, wk), (whole_b, half, wv)], [normed], [[dk], [dv]], gain_acc
    )
    summed = jnp.sum(gain_acc[...], axis=1, keepdims=True)
    gains = lane_column(summed / cols_ref[:, 0:1].astype(F32), 0) + gain_two[...] + gain_three[...]
    whole_a[:, pl.ds(2 * half, PAIR_LANES)] = gains.astype(LOW)
    finish_blocks(packed, (*index, *outs), whole_a, whole_b)


def back_kernel(grads, weight, out):
    out[...] = dot_nt(grads[...], weight[...]).astype(LOW)


def rows_back_kernel(spans, with_query, *refs):
    dk, dv, wk, wv = refs[:4]
    queries = refs[4:6] if with_query else None
    keep, give = refs[-2:]
    rows = dk.shape[0] // len(spans)
    for number, (mine, place) in enumerate(spans):
        at = pl.ds(number * rows, rows)
        value = dot_nt(dk[at, :], wk[...]) + dot_nt(dv[at, :], wv[...])
        if queries and number < 2:
            value = value + dot_nt(queries[0][at, :], queries[1][...])
        if mine:
            keep[place] = value
        else:
            give[place] = value.astype(LOW)


def columns_kernel(place, keep, got, *targets):
    rows = got.shape[0]

    def write(start, first, later):
        for number, target in enumerate(targets):
            half = target.shape[1] // 2
            columns = pl.ds(number * half, half)
            target[:, pl.ds(0, half)] = first(start, columns)
            target[:, pl.ds(half, half)] = later(start, columns)

    from_keep = lambda start, columns: keep[pl.ds(start, rows), columns]
    from_got = lambda start, columns: got[:, columns]

    @pl.when(place[0] == 0)
    def _():
        write(0, from_keep, from_got)

    @pl.when(place[0] != 0)
    def _():
        write(rows, from_got, from_keep)


def after(values, *others):
    return lax.optimization_barrier((values, *others))[0]


def together(*values):
    return lax.optimization_barrier(values)


class Ring:
    def __init__(self):
        self.charts = lax.axis_size("dp")
        self.groups = lax.axis_size("hx")
        self.half = lax.axis_index("hc").astype(jnp.int32)
        self.second = self.half == 1
        self.place = self.half[None]
        self.group = lax.axis_index("hx").astype(jnp.int32)
        self.block = lax.axis_index("dp").astype(jnp.int32) * self.groups + self.group
        self.blocks = self.charts * self.groups
        chart_bits = [("dp", 1 << i) for i in range(self.charts.bit_length() - 1)]
        self.group_bits = [("hx", 1 << i) for i in range(self.groups.bit_length() - 1)]
        self.far = chart_bits[:0:-1]
        near = chart_bits[:1]
        self.tails = (near + self.group_bits, self.group_bits + near)
        self.orders = tuple(self.far + tail for tail in self.tails)

    def send(self, values, axis, bit):
        size = self.charts if axis == "dp" else self.groups
        return lax.ppermute(values, axis, [(i, i ^ bit) for i in range(size)])

    def swap(self, values):
        return lax.ppermute(values, "hc", [(0, 1), (1, 0)])

    def in_order(self, mine, other):
        return jnp.where(self.second, other, mine), jnp.where(self.second, mine, other)

    def steps(self, order):
        return [bit * self.groups if axis == "dp" else bit for axis, bit in order]

    def arrivals(self):
        apart = self.block ^ jnp.arange(self.blocks, dtype=jnp.int32)
        indices = []
        for order in self.orders:
            index = jnp.zeros((self.blocks,), jnp.int32)
            for place, step in enumerate(self.steps(order)):
                index = index + jnp.where((apart & step) != 0, 1 << place, 0)
            indices.append(index)
        return indices

    def origins(self):
        indices = []
        for order in self.orders:
            masks = [0]
            for step in self.steps(order):
                masks = masks + [m ^ step for m in masks]
            indices.append(self.block ^ jnp.asarray(masks, jnp.int32))
        return indices

    def far_step(self, blocks, step):
        return jnp.concatenate([blocks, self.send(blocks, *self.far[step])], axis=0)

    def near_step(self, parts, step):
        return [self.send(part, *tail[step]) for part, tail in zip(parts, self.tails)]

    def near_sends(self, gives, place):
        return [self.send(give, *tail[place]) for give, tail in zip(gives, self.tails)]

    def near_sums(self, keeps, gots):
        add = lambda keep, got: keep.astype(F32) + got.astype(F32)
        for place in reversed(range(len(self.tails[0]))):
            halves = [got.shape[0] // 2 for got in gots]
            kind = LOW if place else F32
            gives = [add(k[h:], g[h:]).astype(kind) for k, g, h in zip(keeps, gots, halves)]
            keeps = [add(k[:h], g[:h]).astype(kind) for k, g, h in zip(keeps, gots, halves)]
            if place:
                gots = self.near_sends(gives, place - 1)
        return jnp.concatenate(keeps, axis=2), jnp.concatenate(gives, axis=2).astype(LOW)

    def far_sum(self, keep, give, step):
        got = self.send(give, *self.far[len(self.far) - 1 - step])
        half = keep.shape[0] // 2
        if not half:
            return keep + got.astype(F32), None
        later = (keep[half:] + got[half:].astype(F32)).astype(LOW)
        return keep[:half] + got[:half].astype(F32), later

    def halve_wholes(self, wholes, rows):
        keeps, gives = [], []
        for whole, index in zip(wholes, self.origins()):
            blocks = jnp.take(whole.reshape(self.blocks, rows, -1), index, axis=0)
            keeps.append(blocks[: self.blocks // 2])
            gives.append(blocks[self.blocks // 2 :])
        return keeps, gives

    def across(self, mine):
        rows = mine[None]
        for axis, bit in self.group_bits:
            rows = jnp.concatenate([rows, self.send(rows, axis, bit)], axis=0)
        return rows

    def halves(self, first, later):
        mine = jnp.where(self.second, later, first)
        give = jnp.where(self.second, first, later)
        return jnp.concatenate(self.in_order(mine, self.swap(give)), axis=0)

    def pair_sum(self, keep, give):
        return keep + self.swap(give.astype(LOW)).astype(F32)

    def group_terms(self, total):
        for axis, bit in reversed(self.group_bits):
            middle = total.shape[0] // 2
            total = total[:middle] + self.send(total[middle:].astype(LOW), axis, bit).astype(F32)
        return total[0]

    def finished(self, keep, count):
        rows = keep.shape[0] // 2
        give = lax.dynamic_slice_in_dim(keep, (1 - self.half) * rows, rows, 0)
        got = self.swap(give)
        width = keep.shape[1] // count * 2
        return run_kernel(
            columns_kernel, [full_shape(rows, width)] * count, rows * width, [self.place], [keep, got]
        )


def column_halves(weights):
    half = weights[0].shape[1] // 2
    return [jnp.concatenate([w[:, i * half : (i + 1) * half] for w in weights], axis=1) for i in range(2)]


def unit_halves(weight, units):
    rows, columns = weight.shape
    split = weight.reshape(rows, columns // (2 * units), 2, units)
    return split[:, :, 0].reshape(rows, -1), split[:, :, 1].reshape(rows, -1)


def unit_whole(first, later, units):
    rows, columns = first.shape
    pieces = [part.reshape(rows, columns // units, 1, units) for part in (first, later)]
    return jnp.concatenate(pieces, axis=2).reshape(rows, 2 * columns)


def on_device(
    tokens,
    memory,
    text_length,
    patch_count,
    self_gain,
    self_query,
    self_key,
    self_value,
    self_out,
    cross_gain,
    cross_query,
    cross_key,
    cross_value,
    cross_out,
    mlp_gain,
    mlp_gate,
    mlp_up,
    mlp_down,
    output_grad,
):
    ring = Ring()
    place = ring.place
    width = tokens.shape[-1]
    half = width // 2
    units = mlp_down.shape[0]
    hidden_half = units * ring.blocks
    rows = self_query.shape[0]
    own = tokens.shape[1]
    own_patches = memory.shape[1]
    both = 2 * own
    keys = both * ring.groups
    patches = 2 * own_patches * ring.groups
    piece = 16
    packed = (2 * rows) % piece == 0 and units == HEAD_DIM and ring.blocks > 1
    pieces, down_pieces = 2 * rows // piece, units // piece
    pairs = ("dp", "hx")
    index_in = tuple(ring.arrivals()) if packed else ()
    index_out = tuple(ring.origins()) if packed else ()
    index_specs = [SMEM_SPEC] * len(index_in)
    block_rows = 2 * rows

    gain_columns = jnp.stack([self_gain, cross_gain, mlp_gain], axis=1)
    gain_columns = jnp.pad(gain_columns, ((0, 0), (0, PAIR_LANES - 3)))
    chains = ([self_query, gain_columns, self_out, cross_query], [self_key, self_value, cross_key, cross_value])
    splits = (half + PAIR_LANES, 2 * half)
    cut_all = 3 * half + PAIR_LANES
    packed_columns = (2 * hidden_half) * pieces + width * down_pieces
    widths_one = ([half, PAIR_LANES], [half, half])
    widths_two = ([half] * 2, [half] * 2)

    if packed:
        kinds = ["all" if w is gain_columns else "half" for w in chains[0] + chains[1]]
        mine, give = cut_shards(place, chains[0] + chains[1], kinds)
        blocks = jnp.concatenate(ring.in_order(mine, ring.swap(give)), axis=0)[None]
    else:
        sides = [
            jnp.concatenate(
                [w if w is gain_columns else column_halves([w])[i] for w in chains[0] + chains[1]],
                axis=1,
            )
            for i in range(2)
        ]
        blocks = ring.halves(*sides)[None]
    middle = own_patches // 2
    blocks = ring.far_step(blocks, 0)
    token_m = ring.across(tokens[0])
    patch_a = ring.across(memory[0, :middle])
    if packed:
        mine, give = cut_shards(place, [mlp_gate, mlp_up, cross_out], ["units"] * 2 + ["half"])
        blocks_mlp = join_rows(place, mine, ring.swap(give), mlp_down, [], half, piece)[0]
    else:
        gate_halves, up_halves = unit_halves(mlp_gate, units), unit_halves(mlp_up, units)
        rest = [
            jnp.concatenate([gate_halves[i], up_halves[i], column_halves([cross_out])[i]], axis=1)
            for i in range(2)
        ]
        gate_up = lax.all_gather(ring.halves(*rest), pairs, axis=0, tiled=True)
        down_three = lax.all_gather(mlp_down, pairs, axis=0, tiled=True)
        out_two = gate_up[:, 2 * hidden_half :]
    blocks, token_m, memory = together(blocks, token_m, memory)
    if packed:
        mlp_weights = lax.all_gather(after(blocks_mlp, blocks), pairs, axis=0, tiled=True)
        mlp_weights = mlp_weights.reshape(ring.blocks, piece, -1)
    patch_b = ring.across(memory[0, middle:])
    for step in range(1, len(ring.far)):
        blocks = ring.far_step(blocks, step)
    blocks, patch_a, token_m = together(blocks, patch_a, token_m)
    parts = [blocks[:, :, :cut_all], blocks[:, :, cut_all:]]
    token_g = ring.swap(token_m)
    last = len(ring.tails[0]) - 1
    for step in range(last):
        got = ring.near_step(parts, step)
        parts = [jnp.concatenate(pair, axis=0) for pair in zip(parts, got)]
    parts, token_g, patch_b = together(parts, token_g, patch_b)
    parts_one = [part[:, :, :split] for part, split in zip(parts, splits)]
    parts_two = [part[:, :, split:] for part, split in zip(parts, splits)]
    near_one = ring.near_step(parts_one, last)
    patch_m = jnp.concatenate([patch_a, patch_b], axis=1)
    patch_g = ring.swap(patch_m)
    near_one, parts_two, patch_g = together(near_one, parts_two, patch_g)
    near_two = ring.near_step(parts_two, last)
    near_one = (parts_one[0], near_one[0], parts_one[1], near_one[1])
    arrivals = ring.arrivals()

    token_chunk = math.gcd(256, own)
    patch_chunk = math.gcd(256, own_patches)

    def chunk_starts(span, chunk, side_first):
        groups = ring.group ^ jnp.arange(ring.groups, dtype=jnp.int32)
        sides = ring.half ^ jnp.arange(2, dtype=jnp.int32)
        inner = jnp.arange(span // chunk, dtype=jnp.int32) * chunk
        if side_first:
            starts = groups[None, :, None] * 2 * span + sides[:, None, None] * span
        else:
            starts = groups[:, None, None] * 2 * span + sides[None, :, None] * span
        return (starts + inner).reshape(-1)

    fixed = jnp.stack([ring.group * both, ring.half])
    info_one = jnp.concatenate([text_length, fixed, chunk_starts(own, token_chunk, False)])
    info_two = jnp.concatenate([patch_count, fixed, chunk_starts(own_patches, patch_chunk, True)])

    head_shapes = [low_shape(both, half), low_shape(keys, half), low_shape(keys, half)]
    query_outs = [full_shape(8, width), low_shape(keys, width), *head_shapes]
    projections = [low_shape(width, w) for w in widths_one[0] + widths_one[1]]
    cost = keys * width * half
    if packed:
        outs = run_kernel(
            functools.partial(query_kernel, True),
            query_outs + projections,
            cost,
            index_in,
            [*near_one, token_m, token_g],
        )
        gain_rows, normed_one, query_heads, key_heads, value_heads = outs[:5]
        query_one, gain_cols, key_one, value_one = outs[5:]
    else:
        query_one, gain_cols = to_whole(near_one[0], near_one[1], arrivals[0], widths_one[0])
        key_one, value_one = to_whole(near_one[2], near_one[3], arrivals[1], widths_one[1])
        gain_rows, normed_one, query_heads, key_heads, value_heads = run_kernel(
            functools.partial(query_kernel, False),
            query_outs,
            cost,
            [],
            [query_one, gain_cols, key_one, value_one, token_m, token_g],
        )
    near_one = None
    grad_g = ring.swap(after(output_grad[0], query_heads))
    context_one, lse_one = attention_forward(
        info_one, query_heads, key_heads, value_heads, True, token_chunk
    )
    context_one, near_b, grad_g = together(context_one, near_two[1], grad_g)
    context_one_g = ring.swap(context_one)
    patch_all = [part.reshape(-1, width) for part in (patch_m, patch_g)]
    memory_heads = [low_shape(patches, half)] * 2
    if packed:
        memory_keys, memory_values, key_two, value_two = run_kernel(
            functools.partial(memory_kernel, True),
            memory_heads + [low_shape(width, half)] * 2,
            patches * width * half,
            index_in[1:],
            [parts_two[1], near_b, *patch_all],
        )
    else:
        key_two, value_two = to_whole(parts_two[1], near_b, arrivals[1], widths_two[1])
        memory_keys, memory_values = run_kernel(
            functools.partial(memory_kernel, False),
            memory_heads,
            patches * width * half,
            [],
            [key_two, value_two, *patch_all],
        )
    near_a, memory_keys = together(near_two[0], memory_keys)
    out_one, query_two = to_whole(parts_two[0], near_a, arrivals[0], widths_two[0])
    out_one_g = ring.swap(out_one)
    hidden_one, normed_two, cross_heads = run_kernel(
        cross_query_kernel,
        [full_shape(both, width), low_shape(both, width), low_shape(both, half)],
        both * width * half,
        [place],
        [token_m[0], token_g[0], context_one, context_one_g, out_one, out_one_g, gain_rows, query_two],
    )
    context_two, lse_two = attention_forward(
        info_two, cross_heads, memory_keys, memory_values, False, patch_chunk
    )
    context_two_g = ring.swap(context_two)
    if packed:
        out_two = from_pieces(after(mlp_weights, context_two), packed_columns, pieces, half)
    out_two_g = ring.swap(out_two)

    if packed:
        hidden_two, part_low, down_keep, down_give, gain_three, mlp_terms = run_kernel(
            functools.partial(mlp_kernel, 512),
            [
                full_shape(both, width),
                low_shape(both, width),
                full_shape(own, width),
                low_shape(own, width),
                full_shape(width, PAIR_LANES),
                low_shape(ring.blocks, piece, packed_columns),
            ],
            2 * both * width * hidden_half,
            [place],
            [
                hidden_one,
                context_two,
                context_two_g,
                out_two,
                out_two_g,
                gain_rows,
                gain_cols,
                output_grad[0],
                grad_g,
            ],
            [
                pltpu.VMEM((ring.blocks, pieces, piece, hidden_half), LOW),
                pltpu.VMEM((ring.blocks, pieces, piece, hidden_half), LOW),
                pltpu.VMEM((ring.blocks, down_pieces, piece, width), LOW),
                pltpu.VMEM((both, width), LOW),
                pltpu.VMEM((width, both), LOW),
                pltpu.VMEM((both, width), LOW),
                pltpu.VMEM((both, width), F32),
                pltpu.VMEM((both, width), F32),
                pltpu.VMEM((width, PAIR_LANES), F32),
                pltpu.SemaphoreType.DMA((2 * pieces + down_pieces,)),
            ],
            [mlp_weights],
            late=True,
        )
        mlp_terms = mlp_terms.reshape(ring.blocks * piece, -1)
        mlp_sum = lax.psum_scatter(mlp_terms, pairs, scatter_dimension=0, tiled=True)
    else:
        joined = jnp.concatenate(ring.in_order(out_two, out_two_g), axis=1)
        swapped = jnp.concatenate([context_two_g[own:], context_two_g[:own]], axis=0)
        context = jnp.concatenate(ring.in_order(context_two, swapped), axis=1)
        hidden_two = hidden_one + dot_nn(context, joined)
        normed_three = (normalize(hidden_two)[0] * gain_rows[2:3]).astype(LOW)
        grad_low = jnp.concatenate([output_grad[0], grad_g], axis=0)
        gate_up = gate_up[:, : 2 * hidden_half]
        gate_three, up_three = gate_up[:, :hidden_half], gate_up[:, hidden_half:]
        active, slope = gelu_parts(dot_nn(normed_three, gate_three))
        up = dot_nn(normed_three, up_three)
        mixed = (active * up).astype(LOW)
        down_part = dot_nn(mixed, down_three)
        down_keep, down_give = down_part[:own], down_part[own:].astype(LOW)
        grad_mixed = dot_nt(grad_low, down_three)
        gate_low = (grad_mixed * up * slope).astype(LOW)
        up_low = (grad_mixed * active).astype(LOW)
        part_low = (dot_nt(gate_low, gate_three) + dot_nt(up_low, up_three)).astype(LOW)
        terms = jnp.concatenate(
            [dot_tn(normed_three, gate_low), dot_tn(normed_three, up_low)], axis=1
        )
        column = jnp.sum(terms * gate_up.astype(F32), axis=1, keepdims=True)
        gain_three = lane_column(column / gain_cols[:, 2:3].astype(F32), 2)
        gate_up = lax.psum_scatter(terms, pairs, scatter_dimension=0, tiled=True)
        mlp_ddown = lax.psum_scatter(
            dot_tn(mixed, grad_low), pairs, scatter_dimension=0, tiled=True
        )

    part_g = ring.swap(part_low)
    down_got = ring.swap(down_give)
    output = (hidden_two[:own] + down_keep + down_got.astype(F32)).astype(LOW)

    def branch(gain_at, hidden, mine, got, weight_m, weight_g, base):
        return run_kernel(
            functools.partial(branch_kernel, gain_at),
            [full_shape(both, width), low_shape(both, width), low_shape(both, half)],
            both * width * half,
            [place],
            [hidden, gain_rows, mine, got, weight_m, weight_g, *base],
        )

    dhidden_two, branch_two, dcontext_two = branch(
        2, hidden_two, part_low, part_g, out_two, out_two_g, [output_grad[0], grad_g]
    )
    dquery, dkey, dvalue = attention_backward(
        info_two,
        cross_heads,
        memory_keys,
        memory_values,
        context_two,
        dcontext_two,
        lse_two,
        False,
        patch_chunk,
    )
    (part_low,) = run_kernel(
        back_kernel, [low_shape(both, width)], both * width, [], [dquery, query_two]
    )
    part_g = ring.swap(part_low)

    count = ring.blocks // 2

    def grads(body, inputs, columns, gain_outs, cost):
        scratch = [pltpu.VMEM((width, c), LOW) for c in columns]
        acc = pltpu.VMEM((width, PAIR_LANES), F32)
        if packed:
            shapes = [low_shape(count, block_rows, c) for c in columns for _ in range(2)]
            outs = run_kernel(
                functools.partial(body, True),
                gain_outs + shapes,
                cost,
                [place, *index_out],
                inputs,
                scratch + [acc],
            )
            blocks = outs[len(gain_outs) :]
            return outs[: len(gain_outs)], blocks[0::2], blocks[1::2]
        wholes = [low_shape(width, c) for c in columns]
        outs = run_kernel(
            functools.partial(body, False), gain_outs + wholes, cost, [place], inputs, [acc]
        )
        return outs[: len(gain_outs)], *ring.halve_wholes(outs[len(gain_outs) :], block_rows)

    (gain_two,), cross_keep, cross_give = grads(
        cross_grads_kernel,
        [
            context_two,
            context_two_g,
            branch_two,
            normed_two,
            dquery,
            *patch_all,
            dkey,
            dvalue,
            query_two,
            gain_cols,
        ],
        (2 * half, 2 * half),
        [full_shape(width, PAIR_LANES)],
        (both + patches) * width * half,
    )
    patch_spans = [(side == 0, g) for side in range(2) for g in range(ring.groups)]
    patch_shape = (ring.groups, own_patches, width)
    memory_keep, memory_give = run_kernel(
        functools.partial(rows_back_kernel, patch_spans, False),
        [full_shape(*patch_shape), low_shape(*patch_shape)],
        patches * width,
        [],
        [dkey, dvalue, key_two, value_two],
    )
    memory_total = ring.pair_sum(memory_keep, memory_give)
    memory_sent = ring.group_terms(memory_total)
    cross_got = ring.near_sends(cross_give, len(ring.tails[0]) - 1)

    dhidden_one, branch_one, dcontext_one = branch(
        1, hidden_one, part_low, part_g, out_one, out_one_g, [dhidden_two]
    )
    dquery_one, dkey_one, dvalue_one = attention_backward(
        info_one,
        query_heads,
        key_heads,
        value_heads,
        context_one,
        dcontext_one,
        lse_one,
        True,
        token_chunk,
    )
    dquery_one, dkey_one, dvalue_one, memory_sent, cross_got = together(
        dquery_one, dkey_one, dvalue_one, memory_sent, cross_got
    )
    memory_grad = memory_sent
    cross_left, cross_give = ring.near_sums(cross_keep, cross_got)
    _, self_keep, self_give = grads(
        self_grads_kernel,
        [
            context_one,
            context_one_g,
            branch_one,
            normed_one,
            dquery_one,
            dkey_one,
            dvalue_one,
            query_one,
            key_one,
            value_one,
            gain_cols,
            gain_two,
            gain_three,
        ],
        (2 * half + PAIR_LANES, 2 * half),
        [],
        (both + keys) * width * half,
    )
    self_got = ring.near_sends(self_give, len(ring.tails[0]) - 1)
    for step in range(len(ring.far)):
        cross_left, cross_give = ring.far_sum(cross_left, cross_give, step)
    cross_sum = cross_left[0]
    self_left, self_give = ring.near_sums(self_keep, self_got)
    late = self_give
    for step in range(len(ring.far)):
        if packed and step == len(ring.far) - 1:
            self_give, mlp_sum = together(self_give, mlp_sum)
        self_left, self_give = ring.far_sum(self_left, self_give, step)
    if packed:
        mlp_sum = mlp_sum.astype(F32)
        take = lambda at, size: mlp_sum[:, at : at + size]
        gate_up = jnp.concatenate(
            [
                jnp.concatenate([take((m * pieces + j) * hidden_half, hidden_half) for m in range(2)], axis=1)
                for j in range(pieces)
            ],
            axis=0,
        )
        base = 2 * pieces * hidden_half
        mlp_ddown = jnp.concatenate(
            [take(base + j * width, width) for j in range(down_pieces)], axis=0
        )

    dquery_one, dkey_one, dvalue_one = after((dquery_one, dkey_one, dvalue_one), self_keep[0])
    token_spans = [(side == 0, g) for g in range(ring.groups) for side in range(2)]
    token_shape = (ring.groups, own, width)
    part_keep, part_give = run_kernel(
        functools.partial(rows_back_kernel, token_spans, True),
        [full_shape(*token_shape), low_shape(*token_shape)],
        keys * width,
        [],
        [dkey_one, dvalue_one, key_one, value_one, dquery_one, query_one],
    )
    dnormed_one = ring.group_terms(after(ring.pair_sum(part_keep, part_give), late))
    plain, inverse = normalize(tokens[0].astype(F32))
    input_grad = dhidden_one[:own] + norm_back(plain, inverse, gain_rows[0:1], dnormed_one)

    (gate_up,) = ring.finished(gate_up, 1)
    gate_columns = [gate_up[:, i * hidden_half : (i + 1) * hidden_half] for i in range(4)]
    mlp_dgate = unit_whole(gate_columns[0], gate_columns[2], units)
    mlp_dup = unit_whole(gate_columns[1], gate_columns[3], units)
    cross_dout, cross_dquery, cross_dkey, cross_dvalue = ring.finished(cross_sum, 4)
    self_left, mlp_dgate, mlp_dup, mlp_ddown = together(self_left, mlp_dgate, mlp_dup, mlp_ddown)
    self_sum = self_left[0]
    gain_at = 2 * half
    gain_block = self_sum[:, gain_at : gain_at + PAIR_LANES]
    gain_block = jnp.pad(gain_block, ((0, 0), (0, half - PAIR_LANES)))
    self_sum = jnp.concatenate(
        [self_sum[:, :gain_at], self_sum[:, gain_at + PAIR_LANES :], gain_block], axis=1
    )
    self_dquery, self_dout, self_dkey, self_dvalue, gain_terms = ring.finished(self_sum, 5)
    dgains = gain_terms[:, :3] + gain_terms[:, half : half + 3]

    return (
        output[None],
        input_grad[None],
        memory_grad[None],
        dgains[:, 0],
        self_dquery,
        self_dkey,
        self_dvalue,
        self_dout,
        dgains[:, 1],
        cross_dquery,
        cross_dkey,
        cross_dvalue,
        cross_dout,
        dgains[:, 2],
        mlp_dgate,
        mlp_dup,
        mlp_ddown,
    )


def solution(mesh):
    charts, heads = mesh.devices.shape
    inner = Mesh(mesh.devices.reshape(charts, heads // 2, 2), ("dp", "hx", "hc"))
    every = ("dp", "hx", "hc")
    rows = P(every, None)
    vector = P(every)
    grid = P("dp", ("hx", "hc"), None)
    in_specs = (grid, grid, P("dp"), P("dp"))
    in_specs += (vector, rows, rows, rows, rows) * 2
    in_specs += (vector, rows, rows, rows, grid)
    out_specs = (grid, grid, grid)
    out_specs += (vector, rows, rows, rows, rows) * 2
    out_specs += (vector, rows, rows, rows)
    return jax.shard_map(
        on_device, mesh=inner, in_specs=in_specs, out_specs=out_specs, check_vma=False
    )
```

profile of v0, /device:TPU:0, one launch (start us, length us, event | category | flops | bytes accessed | tf_op | source)
XLA Modules:
  0.0 364.1 jit_solution(15419641832412468905)
XLA Ops:
  23.5 6.4 %collective-permute-done.1 = bf16[1,48,2816]{2,1,0:T(8,128)(2,1)} collective-permute-done((bf16[1,48,2816]{2,1,0:T(8,128)(2,1)S(1)}, bf16[1,48,2816]{2,1,0:T(8,128)(2,1)}, u32[]{:S(2)}, u32[]{:S(2)}) %collective-permute-start.1) | collective-permute-done | bytes 270368 | tf_op jit(solution)/shard_map/ppermute | solution.py:854
  33.2 9.3 %collective-permute-done.4 = bf16[1,256,768]{2,1,0:T(8,128)(2,1)S(1)} collective-permute-done((bf16[1,256,768]{2,1,0:T(8,128)(2,1)S(1)}, bf16[1,256,768]{2,1,0:T(8,128)(2,1)S(1)}, u32[]{:S(2)}, u32[]{:S(2)}) %collective-permute-start.4) | collective-permute-done | bytes 393248 | tf_op jit(solution)/shard_map/ppermute | solution.py:854
  56.7 15.3 %collective-permute-done.6 = bf16[4,48,1536]{2,1,0:T(8,128)(2,1)S(1)} collective-permute-done((bf16[4,48,1536]{2,1,0:T(8,128)(2,1)S(1)}, bf16[4,48,1536]{2,1,0:T(8,128)(2,1)S(1)}, u32[]{:S(2)}, u32[]{:S(2)}) %collective-permute-start.6) | collective-permute-done | bytes 589856 | tf_op jit(solution)/shard_map/ppermute | solution.py:854
  79.0 8.2 %collective-permute-done.9.refs_3_ = bf16[8,48,512]{2,1,0:T(8,128)(2,1)} collective-permute-done((bf16[8,48,512]{2,1,0:T(8,128)(2,1)}, bf16[8,48,512]{2,1,0:T(8,128)(2,1)}, u32[]{:S(2)}, u32[]{:S(2)}) %collective-permute-start.9) | collective-permute-done | bytes 393248 | tf_op jit(solution)/shard_map/ppermute | solution.py:854
  93.6 7.8 %shard_map.333 = (f32[8,768]{1,0:T(8,128)}, bf16[1024,768]{1,0:T(8,128)(2,1)}, bf16[512,384]{1,0:T(8,128)(2,1)}, bf16[1024,384]{1,0:T(8,128)(2,1)}, bf16[1024,38...) custom-call(s32[16]{0:T(128)} %get-tuple-element.270.refs_0_, ...), custom_call_target="tpu_custom_call" | custom-call | flops 301989 | tf_op jit(solution)/shard_map/pallas_call | solution.py:335
  102.9 8.1 %shard_map.334 = (bf16[512,384]{1,0:T(8,128)(2,1)}, f32[3,2,512]{2,1,0:T(2,128)}) custom-call(s32[7]{0:T(128)} %pad_add_fusion.info, bf16[512,384]{1,0:T(8,128)(2,1)} %get-tuple-element.136.q_ref, bf16[1024,384]{1,0:T(8,128)(2,1)} %get-tuple-element.137.k_ref, bf16[1024,384]{1,0:T(8,128)(2,1)} %get-tuple-element.138.v_ref), custom_call_target="tpu_custom_call" | custom-call | flops 512 | tf_op jit(solution)/shard_map/pallas_call | solution.py:180
  111.0 6.8 %collective-permute-done.12.refs_2_ = bf16[8,48,768]{2,1,0:T(8,128)(2,1)S(1)} collective-permute-done((bf16[8,48,768]{2,1,0:T(8,128)(2,1)}, bf16[8,48,768]{2,1,0:T(8,128)(2,1)S(1)}, u32[]{:S(2)}, u32[]{:S(2)}) %collective-permute-start.12) | collective-permute-done | bytes 589856 | tf_op jit(solution)/shard_map/ppermute | solution.py:854
  118.6 9.0 %shard_map.335 = (bf16[2048,384]{1,0:T(8,128)(2,1)}, bf16[2048,384]{1,0:T(8,128)(2,1)}, bf16[768,384]{1,0:T(8,128)(2,1)}, bf16[768,384]{1,0:T(8,128)(2,1)}) custom-call(s32[16]{0:T(128)} %get-tuple-element.271.refs_1_.refs_0_, bf16[8,48,768]{2,1,0:T(8,128)(2,1)} %get-tuple-element.140.refs_1_, bf16[8,48,768]{2,1,0:T(8,128)(2,1)} %copy-done.27, ...), custom_call_target="tpu_custom_call" | custom-call | flops 603979 | tf_op jit(solution)/shard_map/pallas_call | solution.py:335
  139.6 8.3 %shard_map.338 = (bf16[512,384]{1,0:T(8,128)(2,1)}, f32[3,2,512]{2,1,0:T(2,128)}) custom-call(s32[11]{0:T(128)} %pad_add_fusion.1.info, bf16[512,384]{1,0:T(8,128)(2,1)} %get-tuple-element.152.q_ref, bf16[2048,384]{1,0:T(8,128)(2,1)} %get-tuple-element.153.k_ref, bf16[2048,384]{1,0:T(8,128)(2,1)} %get-tuple-element.154.v_ref), custom_call_target="tpu_custom_call" | custom-call | flops 512 | tf_op jit(solution)/shard_map/pallas_call | solution.py:180
  153.6 16.0 %shard_map.342 = (f32[512,768]{1,0:T(8,128)}, bf16[512,768]{1,0:T(8,128)(2,1)}, f32[256,768]{1,0:T(8,128)}, bf16[256,768]{1,0:T(8,128)(2,1)}, f32[768,128]{1,0:T(8,128)}, /*index=5*/bf16[16,16,9216]{2,1,0:T(8,128)(2,1)}) custom-call(s32[1]{0:T(128)} %bitcast.refs_0_, f32[512,768]{1,0:T(8,128)} %get-tuple-element.151.refs_1_, ...), custom_call_target="tpu_custom_call" | custom-call | flops 805306 | tf_op jit(solution)/shard_map/pallas_call | solution.py:335
  178.8 13.1 %shard_map.344 = (bf16[512,384]{1,0:T(8,128)(2,1)}, bf16[2048,384]{1,0:T(8,128)(2,1)}, bf16[2048,384]{1,0:T(8,128)(2,1)}) custom-call(s32[11]{0:T(128)} %pad_add_fusion.1.info, bf16[512,384]{1,0:T(8,128)(2,1)} %get-tuple-element.152.q_ref, bf16[2048,384]{1,0:T(8,128)(2,1)} %get-tuple-element.153.k_ref, bf16[2048,384]{1,0:T(8,128)(2,1)} %get-tuple-element.154.v_ref, ...), custom_call_target="tpu_custom_call" | custom-call | flops 512 | tf_op jit(solution)/shard_map/pallas_call | solution.py:208
  191.9 6.9 %shard_map.348 = (f32[2,512,768]{2,1,0:T(8,128)}, bf16[2,512,768]{2,1,0:T(8,128)(2,1)}) custom-call(bf16[2048,384]{1,0:T(8,128)(2,1)} %get-tuple-element.176.refs_0_.refs_10_, bf16[2048,384]{1,0:T(8,128)(2,1)} %get-tuple-element.177.refs_1_.refs_11_, bf16[768,384]{1,0:T(8,128)(2,1)} %get-tuple-element.178.refs_2_, bf16[768,384]{1,0:T(8,128)(2,1)} %get-tuple-element.179.refs_3_), custom_call_target="tpu_custom_call" | custom-call | flops 1572 | tf_op jit(solution)/shard_map/pallas_call | solution.py:335
  207.1 10.8 %shard_map.349 = (f32[768,128]{1,0:T(8,128)}, bf16[8,48,768]{2,1,0:T(8,128)(2,1)}, bf16[8,48,768]{2,1,0:T(8,128)(2,1)}, bf16[8,48,768]{2,1,0:T(8,128)(2,1)}, bf16[8,48,768]{2,1,0:T(8,128)(2,1)}) custom-call(s32[1]{0:T(128)} %bitcast.refs_0_, s32[16]{0:T(128)} %get-tuple-element.273.refs_1_, s32[16]{0:T(128)} %get-tuple-element.272.refs_2_, ...), custom_call_target="tpu_custom_call" | custom-call | flops 754974 | tf_op jit(solution)/shard_map/pallas_call | solution.py:335
  218.4 14.5 %collective-permute-start.26 = (bf16[8,48,768]{2,1,0:T(8,128)(2,1)}, bf16[8,48,768]{2,1,0:T(8,128)(2,1)S(1)}, u32[]{:S(2)}, u32[]{:S(2)}) collective-permute-start(bf16[8,48,768]{2,1,0:T(8,128)(2,1)} %get-tuple-element.185), channel_id=1, source_target_pairs={{0,4},{4,0},{8,12},{12,8},{16,20},{20,16},{24,28},{28,24},{1,5},{5... | collective-permute-start | bytes 1769480 | tf_op jit(solution)/shard_map/ppermute | solution.py:854
  234.0 5.1 %shard_map.346 = (f32[512,768]{1,0:T(8,128)}, bf16[512,768]{1,0:T(8,128)(2,1)}, bf16[512,384]{1,0:T(8,128)(2,1)}) custom-call(s32[1]{0:T(128)} %bitcast.refs_0_, f32[512,768]{1,0:T(8,128)} %get-tuple-element.151.refs_1_, f32[8,768]{1,0:T(8,128)} %get-tuple-element.149.refs_7_.refs_6_.refs_2_, bf16[512,768]{1,0:T(8,128)(2,1)} %shard_map.345.refs_3_, ...), custom_call_target="tpu_custom_call" | custom-call | flops 150994 | tf_op jit(solution)/shard_map/pallas_call | solution.py:335
  239.1 12.4 %shard_map.347 = (bf16[512,384]{1,0:T(8,128)(2,1)}, bf16[1024,384]{1,0:T(8,128)(2,1)}, bf16[1024,384]{1,0:T(8,128)(2,1)}) custom-call(s32[7]{0:T(128)} %pad_add_fusion.info, bf16[512,384]{1,0:T(8,128)(2,1)} %get-tuple-element.136.q_ref, bf16[1024,384]{1,0:T(8,128)(2,1)} %get-tuple-element.137.k_ref, bf16[1024,384]{1,0:T(8,128)(2,1)} %get-tuple-element.138.v_ref, ...), custom_call_target="tpu_custom_call" | custom-call | flops 512 | tf_op jit(solution)/shard_map/pallas_call | solution.py:208
  254.4 6.2 %collective-permute-start.37 = (bf16[4,48,768]{2,1,0:T(8,128)(2,1)S(1)}, bf16[4,48,768]{2,1,0:T(8,128)(2,1)S(1)}, u32[]{:S(2)}, u32[]{:S(2)}) collective-permute-start(bf16[4,48,768]{2,1,0:T(8,128)(2,1)S(1)} %get-tuple-element.235), channel_id=1, source_target_pairs={{0,4},{4,0},{8,12},{12,8},{16,20},{20,16},{24,28},{28,24},{1,5},{5... | collective-permute-start | bytes 884744 | tf_op jit(solution)/shard_map/ppermute | solution.py:854
  270.3 8.7 %shard_map.350 = (bf16[8,48,896]{2,1,0:T(8,128)(2,1)}, bf16[8,48,896]{2,1,0:T(8,128)(2,1)}, bf16[8,48,768]{2,1,0:T(8,128)(2,1)}, bf16[8,48,768]{2,1,0:T(8,128)(2,1)}) custom-call(s32[1]{0:T(128)} %bitcast.refs_0_, s32[16]{0:T(128)} %get-tuple-element.273.refs_1_, s32[16]{0:T(128)} %get-tuple-element.272.refs_2_, ...), custom_call_target="tpu_custom_call" | custom-call | flops 452984 | tf_op jit(solution)/shard_map/pallas_call | solution.py:335
  282.0 5.5 %shard_map.351 = (f32[2,256,768]{2,1,0:T(8,128)}, bf16[2,256,768]{2,1,0:T(8,128)(2,1)}) custom-call(bf16[1024,384]{1,0:T(8,128)(2,1)} %get-tuple-element.197.refs_8_.refs_0_, bf16[1024,384]{1,0:T(8,128)(2,1)} %get-tuple-element.198.refs_9_.refs_1_, bf16[768,384]{1,0:T(8,128)(2,1)} %get-tuple-element.192.refs_11_.refs_2_, ...), custom_call_target="tpu_custom_call" | custom-call | flops 786 | tf_op jit(solution)/shard_map/pallas_call | solution.py:335
  287.6 8.8 %collective-permute-start.40 = (bf16[1,48,1536]{2,1,0:T(8,128)(2,1)S(1)}, bf16[1,48,1536]{2,1,0:T(8,128)(2,1)S(1)}, u32[]{:S(2)}, u32[]{:S(2)}) collective-permute-start(bf16[1,48,1536]{2,1,0:T(8,128)(2,1)S(1)} %fusion.19), channel_id=1, source_target_pairs={{0,16},{4,20},{8,24},{12,28},{16,0},{20,4},{24,8},{28,12},{1,17},{... | collective-permute-start | bytes 442376 | tf_op jit(solution)/shard_map/ppermute | solution.py:854
  296.4 5.6 %collective-permute-done.30 = bf16[8,48,768]{2,1,0:T(8,128)(2,1)S(1)} collective-permute-done((bf16[8,48,768]{2,1,0:T(8,128)(2,1)}, bf16[8,48,768]{2,1,0:T(8,128)(2,1)S(1)}, u32[]{:S(2)}, u32[]{:S(2)}) %collective-permute-start.30) | collective-permute-done | bytes 589856 | tf_op jit(solution)/shard_map/ppermute | solution.py:854
  315.9 5.8 %collective-permute-done.33 = bf16[2,48,1664]{2,1,0:T(8,128)(2,1)S(1)} collective-permute-done((bf16[2,48,1664]{2,1,0:T(8,128)(2,1)S(1)}, bf16[2,48,1664]{2,1,0:T(8,128)(2,1)S(1)}, u32[]{:S(2)}, u32[]{:S(2)}) %collective-permute-start.33) | collective-permute-done | bytes 319520 | tf_op jit(solution)/shard_map/ppermute | solution.py:854
  321.8 5.7 %collective-permute-done.32 = bf16[1,256,768]{2,1,0:T(8,128)(2,1)S(1)} collective-permute-done((bf16[1,256,768]{2,1,0:T(8,128)(2,1)S(1)}, bf16[1,256,768]{2,1,0:T(8,128)(2,1)S(1)}, u32[]{:S(2)}, u32[]{:S(2)}) %collective-permute-start.32) | collective-permute-done | bytes 393248 | tf_op jit(solution)/shard_map/ppermute | solution.py:854
  336.9 6.5 %collective-permute-done.34 = bf16[1,48,1664]{2,1,0:T(8,128)(2,1)S(1)} collective-permute-done((bf16[1,48,1664]{2,1,0:T(8,128)(2,1)S(1)}, bf16[1,48,1664]{2,1,0:T(8,128)(2,1)S(1)}, u32[]{:S(2)}, u32[]{:S(2)}) %collective-permute-start.34) | collective-permute-done | bytes 159776 | tf_op jit(solution)/shard_map/ppermute | solution.py:854
  (260 shorter events, 136.8 us)
Async XLA Ops:
  7.2 140.7 %all-gather.2.cloned.1.call-start = ((), (), s32[]{:S(2)}) async-start(), calls=%async_computation.1 | async-start | bytes 5640192 | tf_op jit(solution)/shard_map/all_gather | solution.py:1049
  10.9 12.5 %collective-permute-start.2 = (bf16[1,256,768]{2,1,0:T(8,128)(2,1)}, bf16[1,256,768]{2,1,0:T(8,128)(2,1)S(1)}, u32[]{:S(2)}, u32[]{:S(2)}) collective-permute-start(bf16[1,256,768]{2,1,0:T(8,128)(2,1)} %param.21), channel_id=1, source_target_pairs={{0,2},{2,0},{1,3},{3,1},{4,6},{6,4},{5,7},{7,5},{8,10},{10,8},{9,1... | collective-permute-start | bytes 1179656 | tf_op jit(solution)/shard_map/ppermute | solution.py:854
  14.5 15.4 %collective-permute-start.1 = (bf16[1,48,2816]{2,1,0:T(8,128)(2,1)S(1)}, bf16[1,48,2816]{2,1,0:T(8,128)(2,1)}, u32[]{:S(2)}, u32[]{:S(2)}) collective-permute-start(bf16[1,48,2816]{2,1,0:T(8,128)(2,1)S(1)} %maximum_bitcast_fusion), channel_id=1, source_target_pairs={{0,16},{4,20},{8,24},{12,28},{16,0},{20,4},{24,8},{28,12},{1,17},{... | collective-permute-start | bytes 811016 | tf_op jit(solution)/shard_map/ppermute | solution.py:854
  30.9 301.9 %reduce-scatter.2.cloned.1.call-start = ((), (), s32[]{:S(2)}) async-start(), calls=%async_computation.2 | async-start | bytes 5013504 | tf_op jit(solution)/shard_map/reduce_scatter | solution.py:1197
  30.9 16.0 %collective-permute-start.3 = (bf16[2,48,2816]{2,1,0:T(8,128)(2,1)S(1)}, bf16[2,48,2816]{2,1,0:T(8,128)(2,1)S(1)}, u32[]{:S(2)}, u32[]{:S(2)}) collective-permute-start(bf16[2,48,2816]{2,1,0:T(8,128)(2,1)S(1)} %pad_maximum_fusion.6), channel_id=1, source_target_pairs={{0,8},{4,12},{8,0},{12,4},{16,24},{20,28},{24,16},{28,20},{1,9},{5... | collective-permute-start | bytes 1622024 | tf_op jit(solution)/shard_map/ppermute | solution.py:854
  42.6 12.5 %collective-permute-start.8 = (bf16[1,256,768]{2,1,0:T(8,128)(2,1)S(1)}, bf16[1,256,768]{2,1,0:T(8,128)(2,1)S(1)}, u32[]{:S(2)}, u32[]{:S(2)}) collective-permute-start(bf16[1,256,768]{2,1,0:T(8,128)(2,1)S(1)} %slice.243), channel_id=1, source_target_pairs={{0,2},{2,0},{1,3},{3,1},{4,6},{6,4},{5,7},{7,5},{8,10},{10,8},{9,1... | collective-permute-start | bytes 1179656 | tf_op jit(solution)/shard_map/ppermute | solution.py:854
  48.7 23.3 %collective-permute-start.6 = (bf16[4,48,1536]{2,1,0:T(8,128)(2,1)S(1)}, bf16[4,48,1536]{2,1,0:T(8,128)(2,1)S(1)}, u32[]{:S(2)}, u32[]{:S(2)}) collective-permute-start(bf16[4,48,1536]{2,1,0:T(8,128)(2,1)S(1)} %slice.242), channel_id=1, source_target_pairs={{0,2},{2,0},{1,3},{3,1},{4,6},{6,4},{5,7},{7,5},{8,10},{10,8},{9,1... | collective-permute-start | bytes 1769480 | tf_op jit(solution)/shard_map/ppermute | solution.py:854
  50.2 21.9 %collective-permute-start.7 = (bf16[2,256,768]{2,1,0:T(8,128)(2,1)S(1)}, bf16[2,256,768]{2,1,0:T(8,128)(2,1)S(1)}, u32[]{:S(2)}, u32[]{:S(2)}) collective-permute-start(bf16[2,256,768]{2,1,0:T(8,128)(2,1)S(1)} %pad_maximum_fusion.3.refs_6_), channel_id=1, source_target_pairs={{0,1},{1,0},{2,3},{3,2},{4,5},{5,4},{6,7},{7,6},{8,9},{9,8},{10,11... | collective-permute-start | bytes 2359304 | tf_op jit(solution)/shard_map/ppermute | solution.py:857
  72.2 17.3 %collective-permute-start.11 = (bf16[2,512,768]{2,1,0:T(8,128)(2,1)S(1)}, bf16[2,512,768]{2,1,0:T(8,128)(2,1)S(1)}, u32[]{:S(2)}, u32[]{:S(2)}) collective-permute-start(bf16[2,512,768]{2,1,0:T(8,128)(2,1)S(1)} %constant_dynamic-update-slice_fusion), channel_id=1, source_target_pairs={{0,1},{1,0},{2,3},{3,2},{4,5},{5,4},{6,7},{7,6},{8,9},{9,8},{10,11... | collective-permute-start | bytes 4718600 | tf_op jit(solution)/shard_map/ppermute | solution.py:857
  73.6 15.8 %collective-permute-start.10 = (bf16[8,48,768]{2,1,0:T(8,128)(2,1)}, bf16[8,48,768]{2,1,0:T(8,128)(2,1)}, u32[]{:S(2)}, u32[]{:S(2)}) collective-permute-start(bf16[8,48,768]{2,1,0:T(8,128)(2,1)} %get-tuple-element.239.refs_4_), channel_id=1, source_target_pairs={{0,4},{4,0},{8,12},{12,8},{16,20},{20,16},{24,28},{28,24},{1,5},{5... | collective-permute-start | bytes 1769480 | tf_op jit(solution)/shard_map/ppermute | solution.py:854
  89.4 28.3 %collective-permute-start.12 = (bf16[8,48,768]{2,1,0:T(8,128)(2,1)}, bf16[8,48,768]{2,1,0:T(8,128)(2,1)S(1)}, u32[]{:S(2)}, u32[]{:S(2)}) collective-permute-start(bf16[8,48,768]{2,1,0:T(8,128)(2,1)} %get-tuple-element.140.refs_1_), channel_id=1, source_target_pairs={{0,4},{4,0},{8,12},{12,8},{16,20},{20,16},{24,28},{28,24},{1,5},{5... | collective-permute-start | bytes 1769480 | tf_op jit(solution)/shard_map/ppermute | solution.py:854
  90.9 36.7 %collective-permute-start.15 = (bf16[8,48,768]{2,1,0:T(8,128)(2,1)}, bf16[8,48,768]{2,1,0:T(8,128)(2,1)}, u32[]{:S(2)}, u32[]{:S(2)}) collective-permute-start(bf16[8,48,768]{2,1,0:T(8,128)(2,1)} %slice.247.refs_1_), channel_id=1, source_target_pairs={{0,2},{2,0},{1,3},{3,1},{4,6},{6,4},{5,7},{7,5},{8,10},{10,8},{9,1... | collective-permute-start | bytes 1769480 | tf_op jit(solution)/shard_map/ppermute | solution.py:854
  201.7 31.3 %collective-permute-start.22 = (bf16[512,768]{1,0:T(8,128)(2,1)}, bf16[512,768]{1,0:T(8,128)(2,1)S(1)}, u32[]{:S(2)}, u32[]{:S(2)}) collective-permute-start(bf16[512,768]{1,0:T(8,128)(2,1)} %shard_map.345.refs_3_), channel_id=1, source_target_pairs={{0,1},{1,0},{2,3},{3,2},{4,5},{5,4},{6,7},{7,6},{8,9},{9,8},{10,11... | collective-permute-start | bytes 2359304 | tf_op jit(solution)/shard_map/ppermute | solution.py:857
  204.9 46.7 %collective-permute-start.24 = (bf16[1,512,768]{2,1,0:T(8,128)(2,1)S(1)}, bf16[1,512,768]{2,1,0:T(8,128)(2,1)S(1)}, u32[]{:S(2)}, u32[]{:S(2)}) collective-permute-start(bf16[1,512,768]{2,1,0:T(8,128)(2,1)S(1)} %slice.447), channel_id=1, source_target_pairs={{0,2},{2,0},{1,3},{3,1},{4,6},{6,4},{5,7},{7,5},{8,10},{10,8},{9,1... | collective-permute-start | bytes 2359304 | tf_op jit(solution)/shard_map/ppermute | solution.py:854
  217.9 35.0 %collective-permute-start.25 = (bf16[8,48,768]{2,1,0:T(8,128)(2,1)}, bf16[8,48,768]{2,1,0:T(8,128)(2,1)S(1)}, u32[]{:S(2)}, u32[]{:S(2)}) collective-permute-start(bf16[8,48,768]{2,1,0:T(8,128)(2,1)} %get-tuple-element.184), channel_id=1, source_target_pairs={{0,2},{2,0},{1,3},{3,1},{4,6},{6,4},{5,7},{7,5},{8,10},{10,8},{9,1... | collective-permute-start | bytes 1769480 | tf_op jit(solution)/shard_map/ppermute | solution.py:854
  218.4 34.5 %collective-permute-start.26 = (bf16[8,48,768]{2,1,0:T(8,128)(2,1)}, bf16[8,48,768]{2,1,0:T(8,128)(2,1)S(1)}, u32[]{:S(2)}, u32[]{:S(2)}) collective-permute-start(bf16[8,48,768]{2,1,0:T(8,128)(2,1)} %get-tuple-element.185), channel_id=1, source_target_pairs={{0,4},{4,0},{8,12},{12,8},{16,20},{20,16},{24,28},{28,24},{1,5},{5... | collective-permute-start | bytes 1769480 | tf_op jit(solution)/shard_map/ppermute | solution.py:854
  254.4 13.9 %collective-permute-start.37 = (bf16[4,48,768]{2,1,0:T(8,128)(2,1)S(1)}, bf16[4,48,768]{2,1,0:T(8,128)(2,1)S(1)}, u32[]{:S(2)}, u32[]{:S(2)}) collective-permute-start(bf16[4,48,768]{2,1,0:T(8,128)(2,1)S(1)} %get-tuple-element.235), channel_id=1, source_target_pairs={{0,4},{4,0},{8,12},{12,8},{16,20},{20,16},{24,28},{28,24},{1,5},{5... | collective-permute-start | bytes 884744 | tf_op jit(solution)/shard_map/ppermute | solution.py:854
  260.7 19.7 %collective-permute-start.20 = (bf16[256,768]{1,0:T(8,128)(2,1)S(1)}, bf16[256,768]{1,0:T(8,128)(2,1)S(1)}, u32[]{:S(2)}, u32[]{:S(2)}) collective-permute-start(bf16[256,768]{1,0:T(8,128)(2,1)S(1)} %copy-done.41), channel_id=1, source_target_pairs={{0,1},{1,0},{2,3},{3,2},{4,5},{5,4},{6,7},{7,6},{8,9},{9,8},{10,11... | collective-permute-start | bytes 1179656 | tf_op jit(solution)/shard_map/ppermute | solution.py:857
  268.5 19.1 %collective-permute-start.39 = (bf16[2,48,1536]{2,1,0:T(8,128)(2,1)S(1)}, bf16[2,48,1536]{2,1,0:T(8,128)(2,1)S(1)}, u32[]{:S(2)}, u32[]{:S(2)}) collective-permute-start(bf16[2,48,1536]{2,1,0:T(8,128)(2,1)S(1)} %pad_maximum_fusion.12), channel_id=1, source_target_pairs={{0,8},{4,12},{8,0},{12,4},{16,24},{20,28},{24,16},{28,20},{1,9},{5... | collective-permute-start | bytes 884744 | tf_op jit(solution)/shard_map/ppermute | solution.py:854
  279.0 23.0 %collective-permute-start.30 = (bf16[8,48,768]{2,1,0:T(8,128)(2,1)}, bf16[8,48,768]{2,1,0:T(8,128)(2,1)S(1)}, u32[]{:S(2)}, u32[]{:S(2)}) collective-permute-start(bf16[8,48,768]{2,1,0:T(8,128)(2,1)} %get-tuple-element.204), channel_id=1, source_target_pairs={{0,4},{4,0},{8,12},{12,8},{16,20},{20,16},{24,28},{28,24},{1,5},{5... | collective-permute-start | bytes 1769480 | tf_op jit(solution)/shard_map/ppermute | solution.py:854
  281.2 21.7 %collective-permute-start.28 = (bf16[8,48,896]{2,1,0:T(8,128)(2,1)S(1)}, bf16[8,48,896]{2,1,0:T(8,128)(2,1)S(1)}, u32[]{:S(2)}, u32[]{:S(2)}) collective-permute-start(bf16[8,48,896]{2,1,0:T(8,128)(2,1)S(1)} %copy-done.40), channel_id=1, source_target_pairs={{0,2},{2,0},{1,3},{3,1},{4,6},{6,4},{5,7},{7,5},{8,10},{10,8},{9,1... | collective-permute-start | bytes 2064392 | tf_op jit(solution)/shard_map/ppermute | solution.py:854
  287.5 24.8 %collective-permute-start.27 = (bf16[2,256,768]{2,1,0:T(8,128)(2,1)}, bf16[2,256,768]{2,1,0:T(8,128)(2,1)S(1)}, u32[]{:S(2)}, u32[]{:S(2)}) collective-permute-start(bf16[2,256,768]{2,1,0:T(8,128)(2,1)} %get-tuple-element.201), channel_id=1, source_target_pairs={{0,1},{1,0},{2,3},{3,2},{4,5},{5,4},{6,7},{7,6},{8,9},{9,8},{10,11... | collective-permute-start | bytes 2359304 | tf_op jit(solution)/shard_map/ppermute | solution.py:857
  287.6 21.4 %collective-permute-start.40 = (bf16[1,48,1536]{2,1,0:T(8,128)(2,1)S(1)}, bf16[1,48,1536]{2,1,0:T(8,128)(2,1)S(1)}, u32[]{:S(2)}, u32[]{:S(2)}) collective-permute-start(bf16[1,48,1536]{2,1,0:T(8,128)(2,1)S(1)} %fusion.19), channel_id=1, source_target_pairs={{0,16},{4,20},{8,24},{12,28},{16,0},{20,4},{24,8},{28,12},{1,17},{... | collective-permute-start | bytes 442376 | tf_op jit(solution)/shard_map/ppermute | solution.py:854
  314.9 12.6 %collective-permute-start.32 = (bf16[1,256,768]{2,1,0:T(8,128)(2,1)S(1)}, bf16[1,256,768]{2,1,0:T(8,128)(2,1)S(1)}, u32[]{:S(2)}, u32[]{:S(2)}) collective-permute-start(bf16[1,256,768]{2,1,0:T(8,128)(2,1)S(1)} %slice.448), channel_id=1, source_target_pairs={{0,2},{2,0},{1,3},{3,1},{4,6},{6,4},{5,7},{7,5},{8,10},{10,8},{9,1... | collective-permute-start | bytes 1179656 | tf_op jit(solution)/shard_map/ppermute | solution.py:854
  (62 other events, 380.5 us)
Sparse Core Ops, SparseCore 0:
  31.0 106.5 all-gather.1
  169.7 162.9 reduce-scatter.1
where the time goes:
time: 368 us; the launch traced here: 364 us
  Pallas kernels  140 us (38%)
  waiting for transfers between devices  105 us (29%)
  starting transfers between devices  63.2 us (17%)
  local copies, waits for them, and re-layouts  24.3 us (7%)
  between operations  16.5 us (4%)
  other arithmetic  14.4 us (4%)
    pallas_call x18, Pallas kernels, run_kernel(): pl.pallas_call(functools.partial(staged_kernel, body, late, sizes), out_s...  96.2 us
    ppermute x25, waiting for transfers between devices, send(): return lax.ppermute(values, axis, [(i, i ^ bit) for i in range(size)])  94.3 us
    ppermute x25, starting transfers between devices, send(): return lax.ppermute(values, axis, [(i, i ^ bit) for i in range(size)])  60.1 us
    pallas_call x2, Pallas kernels, attention_backward(): pl.pallas_call(functools.partial(backward_kernel, causal, chunk, span), o...  25.6 us
    pallas_call x2, Pallas kernels, attention_forward(): pl.pallas_call(functools.partial(forward_kernel, causal, chunk, span), ou...  16.4 us
    unnamed x85, local copies, waits for them, and re-layouts  9.86 us
  transfers between devices with their start and end apart: 44, of which 23 were waited for; matrix products, arithmetic and copies ran while one was open for 5% of the time, Pallas kernels for 32%

commit v1 on v0

--- a/solution.py
+++ b/solution.py
@@ -294,33 +294,44 @@
     )
 
 
+class Stage:
+    def __init__(self, loads, stores):
+        self.loads, self.stores = loads, stores
+        self.waited, self.sent = set(), set()
+
+    def need(self, *numbers):
+        for i in numbers or range(len(self.loads)):
+            if i not in self.waited:
+                self.waited.add(i)
+                self.loads[i].wait()
+
+    def done(self, *numbers):
+        for i in numbers or range(len(self.stores)):
+            if i not in self.sent:
+                self.sent.add(i)
+                self.stores[i].start()
+
+
 def staged_kernel(body, late, sizes, *refs):
     parts, at = [], 0
     for size in sizes:
         parts.append(refs[at : at + size])
         at += size
     tables, arrays, streamed, outs, scratch, held_in, held_out, (in_sems, out_sems) = parts
-    loads = [
-        pltpu.make_async_copy(a, b, in_sems.at[i]) for i, (a, b) in enumerate(zip(arrays, held_in))
-    ]
-    for load in loads:
+    stage = Stage(
+        [pltpu.make_async_copy(a, b, in_sems.at[i]) for i, (a, b) in enumerate(zip(arrays, held_in))],
+        [pltpu.make_async_copy(a, b, out_sems.at[i]) for i, (a, b) in enumerate(zip(held_out, outs))],
+    )
+    for load in stage.loads:
         load.start()
-
-    def ready():
-        for load in loads:
-            load.wait()
-
     if late:
-        body(ready, *tables, *held_in, *streamed, *held_out, *scratch)
+        body(stage, *tables, *held_in, *streamed, *held_out, *scratch)
     else:
-        ready()
+        stage.need()
         body(*tables, *held_in, *streamed, *held_out, *scratch)
-    stores = [
-        pltpu.make_async_copy(a, b, out_sems.at[i]) for i, (a, b) in enumerate(zip(held_out, outs))
-    ]
-    for store in stores:
-        store.start()
-    for store in stores:
+    stage.need()
+    stage.done()
+    for store in stage.stores:
         store.wait()
 
 
@@ -508,30 +519,35 @@
     return mine, other
 
 
-def project_heads(gain_cols, token_m, token_g, weights, rows_ref, normed_ref, heads):
-    gain_rows = gain_cols.astype(F32).T[0:8]
+def query_kernel(packed, stage, *refs):
+    if packed:
+        index_a, index_b, first_a, later_a, first_b, later_b, token_m, token_g = refs[:8]
+        rows_ref, normed_ref, q_ref, k_ref, v_ref, wq, gain_cols, wkv = refs[8:]
+        stage.need(0, 1)
+        place_blocks(index_a, first_a, later_a, [wq, gain_cols])
+        stage.done(5, 6)
+        stage.need(2, 3)
+        place_blocks(index_b, first_b, later_b, [wkv])
+        stage.done(7)
+    else:
+        wq, gain_cols, wkv, token_m, token_g = refs[:5]
+        rows_ref, normed_ref, q_ref, k_ref, v_ref = refs[5:]
+    stage.need()
+    gain_rows = gain_cols[...].astype(F32).T[0:8]
     rows_ref[...] = gain_rows
     groups, own, _ = token_m.shape
+    half = q_ref.shape[1]
     for group in range(groups):
         for side, source in enumerate((token_m, token_g)):
             plain, _ = normalize(source[group].astype(F32))
             at = pl.ds((2 * group + side) * own, own)
             normed_ref[at, :] = (plain * gain_rows[0:1]).astype(LOW)
-    for number, (weight, target) in enumerate(zip(weights, heads)):
-        target[...] = dot_nn(normed_ref[pl.ds(0, target.shape[0]), :], weight[...]).astype(LOW)
-
-
-def query_kernel(packed, *refs):
-    if packed:
-        index_a, index_b, first_a, later_a, first_b, later_b, token_m, token_g = refs[:8]
-        rows_ref, normed_ref, q_ref, k_ref, v_ref, wq, gain_cols, wk, wv = refs[8:]
-        place_blocks(index_a, first_a, later_a, [wq, gain_cols])
-        place_blocks(index_b, first_b, later_b, [wk, wv])
-    else:
-        wq, gain_cols, wk, wv, token_m, token_g = refs[:6]
-        rows_ref, normed_ref, q_ref, k_ref, v_ref = refs[6:]
-    heads = (q_ref, k_ref, v_ref)
-    project_heads(gain_cols[...], token_m, token_g, (wq, wk, wv), rows_ref, normed_ref, heads)
+    stage.done(0, 1)
+    q_ref[...] = dot_nn(normed_ref[pl.ds(0, 2 * own), :], wq[...]).astype(LOW)
+    stage.done(2)
+    value = dot_nn(normed_ref[...], wkv[...]).astype(LOW)
+    k_ref[...] = value[:, :half]
+    v_ref[...] = value[:, half:]
 
 
 def add_context(place, target, base, c_m, c_g, w_m, w_g):
@@ -547,31 +563,34 @@
             target[at, columns] = base(side, columns) + value
 
 
-def cross_query_kernel(place, token_m, token_g, c_m, c_g, w_m, w_g, rows_ref, wq, h_ref, normed_ref, q_ref):
+def cross_query_kernel(stage, place, token_m, token_g, c_m, c_g, w_m, w_g, rows_ref, wq, h_ref, normed_ref, q_ref):
     tokens = (token_m, token_g)
     base = lambda side, columns: tokens[side][:, columns].astype(F32)
+    stage.need(*range(7))
     add_context(place, h_ref, base, c_m, c_g, w_m, w_g)
+    stage.done(0)
     plain, _ = normalize(h_ref[...])
     normed_ref[...] = (plain * rows_ref[1:2, :]).astype(LOW)
+    stage.done(1)
+    stage.need()
     q_ref[...] = dot_nn(normed_ref[...], wq[...]).astype(LOW)
 
 
-def memory_kernel(packed, *refs):
+def memory_kernel(packed, stage, *refs):
     if packed:
-        index, first, later, patch_m, patch_g, k_ref, v_ref, wk, wv = refs
-        place_blocks(index, first, later, [wk, wv])
+        index, first, later, patch_m, patch_g, k_ref, v_ref, wkv = refs
+        stage.need(0, 1)
+        place_blocks(index, first, later, [wkv])
+        stage.done(2)
     else:
-        wk, wv, patch_m, patch_g, k_ref, v_ref = refs
+        wkv, patch_m, patch_g, k_ref, v_ref = refs
+    stage.need()
     count = patch_m.shape[0]
-    step = math.gcd(count, 512)
+    half = k_ref.shape[1]
     for side, source in enumerate((patch_m, patch_g)):
-
-        @pl.loop(0, count // step)
-        def _(number):
-            part = source[pl.ds(pl.multiple_of(number * step, step), step), :]
-            place = pl.ds(pl.multiple_of(side * count + number * step, step), step)
-            k_ref[place, :] = dot_nn(part, wk[...]).astype(LOW)
-            v_ref[place, :] = dot_nn(part, wv[...]).astype(LOW)
+        value = dot_nn(source[...], wkv[...]).astype(LOW)
+        k_ref[pl.ds(side * count, count), :] = value[:, :half]
+        v_ref[pl.ds(side * count, count), :] = value[:, half:]
 
 
 def lane_column(column, lane):
@@ -581,7 +600,7 @@
 
 def mlp_kernel(
     chunk,
-    ready,
+    stage,
     place,
     h_in,
     c_m,
@@ -625,13 +644,15 @@
     copies = [pltpu.make_async_copy(a, b, sems.at[i]) for i, (a, b) in enumerate(moves)]
     for copy in copies:
         copy.start()
-    ready()
+    stage.need(*range(6))
     add_context(
         place, h_ref, lambda side, columns: h_in[pl.ds(side * own, own), columns], c_m, c_g, out_m, out_g
     )
+    stage.done(0)
     plain, _ = normalize(h_ref[...])
     a_ref[...] = (plain * rows_ref[2:3, :]).astype(LOW)
     t_ref[...] = a_ref[...].T
+    stage.need()
     g_ref[pl.ds(0, own), :] = g_m[...]
     g_ref[pl.ds(own, own), :] = g_g[...]
     p_acc[...] = jnp.zeros(p_acc.shape, F32)
@@ -678,20 +699,23 @@
         for number in range(down_pieces):
             grad_ref[down_at, :, pl.ds(base + number * width, width)] = ddown[:, number]
 
+    stage.done(5)
     part_ref[...] = p_acc[...].astype(LOW)
+    stage.done(1)
     keep_ref[...] = d_acc[pl.ds(0, own), :]
     give_ref[...] = d_acc[pl.ds(own, own), :].astype(LOW)
     summed = jnp.sum(r_acc[...], axis=1, keepdims=True)
     gain_ref[...] = lane_column(summed / cols_ref[:, 2:3].astype(F32), 2)
 
 
-def branch_kernel(gain_at, place, *refs):
+def branch_kernel(gain_at, stage, place, *refs):
     h_ref, rows_ref, part_m, part_g, w_m, w_g = refs[:6]
     base, (d_ref, low_ref, c_ref) = refs[6:-3], refs[-3:]
     rows = h_ref.shape[0]
     own = rows // 2
     half = w_m.shape[1]
     mine, other = head_slices(place, half)
+    stage.need(0, 1, 2, 3, *range(6, 6 + len(base)))
     for side in range(2):
         at = pl.ds(side * own, own)
         plain, inverse = normalize(h_ref[at, :])
@@ -700,7 +724,10 @@
         value = norm_back(plain, inverse, rows_ref[gain_at : gain_at + 1, :], grads)
         before = base[side][...].astype(F32) if len(base) == 2 else base[0][at, :]
         d_ref[at, :] = before + value
+    stage.done(0)
     low_ref[...] = d_ref[...].astype(LOW)
+    stage.done(1)
+    stage.need()
     value = dot_nt(low_ref[:, mine], w_m[mine, :]) + dot_nt(low_ref[:, other], w_g[mine, :])
     c_ref[...] = value.astype(LOW)
 
@@ -740,46 +767,52 @@
                 )
 
 
-def finish_blocks(packed, refs, whole_a, whole_b):
-    if packed:
-        index_a, index_b, keep_a, give_a, keep_b, give_b = refs
-        send_order(index_a, whole_a, keep_a, give_a)
-        send_order(index_b, whole_b, keep_b, give_b)
-
-
-def cross_grads_kernel(packed, place, *refs):
+def cross_grads_kernel(packed, stage, place, *refs):
     index, refs = (refs[:2], refs[2:]) if packed else ((), refs)
     c_m, c_g, branch, normed, dq, patch_m, patch_g, dk, dv, wq, cols_ref = refs[:11]
-    gain_ref, *outs, whole_a, whole_b, gain_acc = refs[11:]
+    one_m, one_g, branch_one = refs[11:14]
+    gain_ref, *outs, whole_a, whole_b, gain_acc = refs[14:]
     half = dq.shape[1]
+    stage.need(0, 1, 2, 3, 4, 9, 10, 11, 12, 13)
+    out_grad(place, whole_a, 2 * half, one_m, one_g, branch_one)
     count = patch_m.shape[0]
     gain_acc[...] = jnp.zeros(gain_acc.shape, F32)
     out_grad(place, whole_a, 0, c_m, c_g, branch)
     weight_grads([(whole_a, half, wq)], [normed], [[dq]], gain_acc)
+    if packed:
+        send_order(index[0], whole_a, outs[0], outs[1])
+        stage.done(1, 2)
+    summed = jnp.sum(gain_acc[...], axis=1, keepdims=True)
+    gain_ref[...] = lane_column(summed / cols_ref[:, 1:2].astype(F32), 1)
+    stage.need()
     halves = [[g.at[pl.ds(i * count, count), :] for i in range(2)] for g in (dk, dv)]
     weight_grads(
         [(whole_b, 0, None), (whole_b, half, None)], [patch_m, patch_g], halves
     )
-    summed = jnp.sum(gain_acc[...], axis=1, keepdims=True)
-    gain_ref[...] = lane_column(summed / cols_ref[:, 1:2].astype(F32), 1)
-    finish_blocks(packed, (*index, *outs), whole_a, whole_b)
-
-
-def self_grads_kernel(packed, place, *refs):
+    if packed:
+        send_order(index[1], whole_b, outs[2], outs[3])
+
+
+def self_grads_kernel(packed, stage, place, *refs):
     index, refs = (refs[:2], refs[2:]) if packed else ((), refs)
-    c_m, c_g, branch, normed, dq, dk, dv, wq, wk, wv, cols_ref, gain_two, gain_three = refs[:13]
-    *outs, whole_a, whole_b, gain_acc = refs[13:]
+    normed, dq, dk, dv, wq, wkv, cols_ref, gain_two, gain_three = refs[:9]
+    *outs, whole_a, whole_b, gain_acc = refs[9:]
     rows, half = dq.shape
     gain_acc[...] = jnp.zeros(gain_acc.shape, F32)
+    stage.need(0, 3, 5)
+    weight_grads([(whole_b, 0, wkv.at[:, pl.ds(half, half)])], [normed], [[dv]], gain_acc)
+    stage.need(2)
+    weight_grads([(whole_b, half, wkv.at[:, pl.ds(0, half)])], [normed], [[dk]], gain_acc)
+    if packed:
+        send_order(index[1], whole_b, outs[2], outs[3])
+        stage.done(2, 3)
+    stage.need()
     weight_grads([(whole_a, 0, wq)], [normed.at[pl.ds(0, rows), :]], [[dq]], gain_acc)
-    out_grad(place, whole_a, half, c_m, c_g, branch)
-    weight_grads(
-        [(whole_b, 0, wk), (whole_b, half, wv)], [normed], [[dk], [dv]], gain_acc
-    )
     summed = jnp.sum(gain_acc[...], axis=1, keepdims=True)
     gains = lane_column(summed / cols_ref[:, 0:1].astype(F32), 0) + gain_two[...] + gain_three[...]
-    whole_a[:, pl.ds(2 * half, PAIR_LANES)] = gains.astype(LOW)
-    finish_blocks(packed, (*index, *outs), whole_a, whole_b)
+    whole_a[:, pl.ds(half, PAIR_LANES)] = gains.astype(LOW)
+    if packed:
+        send_order(index[0], whole_a, outs[0], outs[1])
 
 
 def back_kernel(grads, weight, out):
@@ -787,8 +820,10 @@
 
 
 def rows_back_kernel(spans, with_query, *refs):
-    dk, dv, wk, wv = refs[:4]
-    queries = refs[4:6] if with_query else None
+    dk, dv, wkv = refs[:3]
+    queries = refs[3:5] if with_query else None
+    half = dk.shape[1]
+    wk, wv = wkv.at[:, pl.ds(0, half)], wkv.at[:, pl.ds(half, half)]
     keep, give = refs[-2:]
     rows = dk.shape[0] // len(spans)
     for number, (mine, place) in enumerate(spans):
@@ -800,6 +835,39 @@
             keep[place] = value
         else:
             give[place] = value.astype(LOW)
+
+
+def feed_forward_grads_kernel(pieces, units, place, sums, got, gate_ref, up_ref, down_ref):
+    piece = sums.shape[0]
+    rows = got.shape[0]
+    hidden = got.shape[1] // 2
+    step = 8
+
+    def write(second):
+        for row in range(0, rows, step):
+            at = row + (rows if second else 0)
+            number, inner = at // piece, at % piece
+            for matrix, target in enumerate((gate_ref, up_ref)):
+                start = (matrix * pieces + number) * hidden
+                mine = sums[pl.ds(inner, step), pl.ds(start, hidden)].astype(F32)
+                other = got[pl.ds(row, step), pl.ds(matrix * hidden, hidden)].astype(F32)
+                pair = (other, mine) if second else (mine, other)
+                for unit in range(0, hidden, units):
+                    tile = jnp.concatenate([part[:, unit : unit + units] for part in pair], axis=1)
+                    target[pl.ds(row, step), pl.ds(2 * unit, 2 * units)] = tile
+
+    @pl.when(place[0] == 0)
+    def _():
+        write(False)
+
+    @pl.when(place[0] != 0)
+    def _():
+        write(True)
+
+    base = 2 * pieces * hidden
+    width = down_ref.shape[1]
+    for number in range(down_ref.shape[0] // piece):
+        down_ref[pl.ds(number * piece, piece), :] = sums[:, pl.ds(base + number * width, width)].astype(F32)
 
 
 def columns_kernel(place, keep, got, *targets):
@@ -881,6 +949,12 @@
             indices.append(self.block ^ jnp.asarray(masks, jnp.int32))
         return indices
 
+    def far_masks(self):
+        masks = [0]
+        for _, bit in self.far:
+            masks = masks + [m | bit for m in masks]
+        return masks
+
     def far_step(self, blocks, step):
         return jnp.concatenate([blocks, self.send(blocks, *self.far[step])], axis=0)
 
@@ -890,24 +964,46 @@
     def near_sends(self, gives, place):
         return [self.send(give, *tail[place]) for give, tail in zip(gives, self.tails)]
 
-    def near_sums(self, keeps, gots):
-        add = lambda keep, got: keep.astype(F32) + got.astype(F32)
-        for place in reversed(range(len(self.tails[0]))):
-            halves = [got.shape[0] // 2 for got in gots]
-            kind = LOW if place else F32
-            gives = [add(k[h:], g[h:]).astype(kind) for k, g, h in zip(keeps, gots, halves)]
-            keeps = [add(k[:h], g[:h]).astype(kind) for k, g, h in zip(keeps, gots, halves)]
-            if place:
-                gots = self.near_sends(gives, place - 1)
-        return jnp.concatenate(keeps, axis=2), jnp.concatenate(gives, axis=2).astype(LOW)
-
-    def far_sum(self, keep, give, step):
-        got = self.send(give, *self.far[len(self.far) - 1 - step])
-        half = keep.shape[0] // 2
-        if not half:
-            return keep + got.astype(F32), None
-        later = (keep[half:] + got[half:].astype(F32)).astype(LOW)
-        return keep[:half] + got[:half].astype(F32), later
+    def near_sums(self, keeps, gots, place):
+        halves = [got.shape[0] // 2 for got in gots]
+        add = lambda k, g: (k.astype(F32) + g.astype(F32)).astype(LOW)
+        gives = [add(k[h:], g[h:]) for k, g, h in zip(keeps, gots, halves)]
+        keeps = [add(k[:h], g[:h]) for k, g, h in zip(keeps, gots, halves)]
+        return keeps, gives
+
+    def far_sends(self, keeps, gots):
+        count = 1 << len(self.far)
+        add = lambda r: [
+            k[r : r + 1].astype(F32) + g[r : r + 1].astype(F32) for k, g in zip(keeps, gots)
+        ]
+        block = lambda r: jnp.concatenate(add(r), axis=2)
+        if len(self.far) == 2:
+            masks = self.far_masks()
+            return block(0), [self.send(block(r).astype(LOW), "dp", masks[r]) for r in range(1, count)]
+        keep = jnp.concatenate([block(r) for r in range(count)], axis=0)
+        for axis, bit in reversed(self.far[1:]):
+            half = keep.shape[0] // 2
+            keep = keep[:half] + self.send(keep[half:].astype(LOW), axis, bit).astype(F32)
+        return keep[:1], [self.send(keep[1:].astype(LOW), *self.far[0])]
+
+    def far_sum(self, own, gots):
+        return sum((got.astype(F32) for got in gots), own)[0]
+
+    def far_first(self, keeps, gots):
+        count = 1 << len(self.far)
+        add = lambda r: jnp.concatenate(
+            [k[r].astype(F32) + g[r].astype(F32) for k, g in zip(keeps, gots)], axis=2
+        )
+        keep, give = add(slice(0, count // 2)), add(slice(count // 2, None)).astype(LOW)
+        return keep, self.send(give, *self.far[-1])
+
+    def far_last(self, keep, got):
+        for axis, bit in reversed(self.far[:-1]):
+            half = keep.shape[0] // 2
+            give = (keep[half:] + got[half:].astype(F32)).astype(LOW)
+            keep = keep[:half] + got[:half].astype(F32)
+            got = self.send(give, axis, bit)
+        return keep, [got]
 
     def halve_wholes(self, wholes, rows):
         keeps, gives = [], []
@@ -1012,8 +1108,8 @@
     splits = (half + PAIR_LANES, 2 * half)
     cut_all = 3 * half + PAIR_LANES
     packed_columns = (2 * hidden_half) * pieces + width * down_pieces
-    widths_one = ([half, PAIR_LANES], [half, half])
-    widths_two = ([half] * 2, [half] * 2)
+    widths_one = ([half, PAIR_LANES], [width])
+    widths_two = ([half] * 2, [width])
 
     if packed:
         kinds = ["all" if w is gain_columns else "half" for w in chains[0] + chains[1]]
@@ -1029,11 +1125,11 @@
         ]
         blocks = ring.halves(*sides)[None]
     middle = own_patches // 2
-    blocks = ring.far_step(blocks, 0)
     token_m = ring.across(tokens[0])
     patch_a = ring.across(memory[0, :middle])
     if packed:
-        mine, give = cut_shards(place, [mlp_gate, mlp_up, cross_out], ["units"] * 2 + ["half"])
+        rest = after([mlp_gate, mlp_up, cross_out], blocks)
+        mine, give = cut_shards(place, rest, ["units"] * 2 + ["half"])
         blocks_mlp = join_rows(place, mine, ring.swap(give), mlp_down, [], half, piece)[0]
     else:
         gate_halves, up_halves = unit_halves(mlp_gate, units), unit_halves(mlp_up, units)
@@ -1044,6 +1140,7 @@
         gate_up = lax.all_gather(ring.halves(*rest), pairs, axis=0, tiled=True)
         down_three = lax.all_gather(mlp_down, pairs, axis=0, tiled=True)
         out_two = gate_up[:, 2 * hidden_half :]
+    blocks = ring.far_step(blocks, 0)
     blocks, token_m, memory = together(blocks, token_m, memory)
     if packed:
         mlp_weights = lax.all_gather(after(blocks_mlp, blocks), pairs, axis=0, tiled=True)
@@ -1097,63 +1194,68 @@
             cost,
             index_in,
             [*near_one, token_m, token_g],
+            late=True,
         )
         gain_rows, normed_one, query_heads, key_heads, value_heads = outs[:5]
-        query_one, gain_cols, key_one, value_one = outs[5:]
+        query_one, gain_cols, heads_one = outs[5:]
     else:
         query_one, gain_cols = to_whole(near_one[0], near_one[1], arrivals[0], widths_one[0])
-        key_one, value_one = to_whole(near_one[2], near_one[3], arrivals[1], widths_one[1])
+        (heads_one,) = to_whole(near_one[2], near_one[3], arrivals[1], widths_one[1])
         gain_rows, normed_one, query_heads, key_heads, value_heads = run_kernel(
             functools.partial(query_kernel, False),
             query_outs,
             cost,
             [],
-            [query_one, gain_cols, key_one, value_one, token_m, token_g],
+            [query_one, gain_cols, heads_one, token_m, token_g],
+            late=True,
         )
     near_one = None
     grad_g = ring.swap(after(output_grad[0], query_heads))
     context_one, lse_one = attention_forward(
         info_one, query_heads, key_heads, value_heads, True, token_chunk
     )
-    context_one, near_b, grad_g = together(context_one, near_two[1], grad_g)
+    context_one, near_a, near_b, grad_g = together(context_one, *near_two, grad_g)
     context_one_g = ring.swap(context_one)
+    out_one, query_two = to_whole(parts_two[0], near_a, arrivals[0], widths_two[0])
+    out_one_g = ring.swap(out_one)
     patch_all = [part.reshape(-1, width) for part in (patch_m, patch_g)]
     memory_heads = [low_shape(patches, half)] * 2
     if packed:
-        memory_keys, memory_values, key_two, value_two = run_kernel(
+        memory_keys, memory_values, heads_two = run_kernel(
             functools.partial(memory_kernel, True),
-            memory_heads + [low_shape(width, half)] * 2,
+            memory_heads + [low_shape(width, width)],
             patches * width * half,
             index_in[1:],
             [parts_two[1], near_b, *patch_all],
+            late=True,
         )
     else:
-        key_two, value_two = to_whole(parts_two[1], near_b, arrivals[1], widths_two[1])
+        (heads_two,) = to_whole(parts_two[1], near_b, arrivals[1], widths_two[1])
         memory_keys, memory_values = run_kernel(
             functools.partial(memory_kernel, False),
             memory_heads,
             patches * width * half,
             [],
-            [key_two, value_two, *patch_all],
+            [heads_two, *patch_all],
+            late=True,
         )
-    near_a, memory_keys = together(near_two[0], memory_keys)
-    out_one, query_two = to_whole(parts_two[0], near_a, arrivals[0], widths_two[0])
-    out_one_g = ring.swap(out_one)
+    context_one_g, memory_keys = together(context_one_g, memory_keys)
     hidden_one, normed_two, cross_heads = run_kernel(
         cross_query_kernel,
         [full_shape(both, width), low_shape(both, width), low_shape(both, half)],
         both * width * half,
         [place],
         [token_m[0], token_g[0], context_one, context_one_g, out_one, out_one_g, gain_rows, query_two],
-    )
+        late=True,
+    )
+    if packed:
+        out_two = from_pieces(after(mlp_weights, cross_heads), packed_columns, pieces, half)
+    cross_heads, out_two = together(cross_heads, out_two)
+    out_two_g = ring.swap(out_two)
     context_two, lse_two = attention_forward(
         info_two, cross_heads, memory_keys, memory_values, False, patch_chunk
     )
     context_two_g = ring.swap(context_two)
-    if packed:
-        out_two = from_pieces(after(mlp_weights, context_two), packed_columns, pieces, half)
-    out_two_g = ring.swap(out_two)
-
     if packed:
         hidden_two, part_low, down_keep, down_give, gain_three, mlp_terms = run_kernel(
             functools.partial(mlp_kernel, 512),
@@ -1234,6 +1336,7 @@
             both * width * half,
             [place],
             [hidden, gain_rows, mine, got, weight_m, weight_g, *base],
+            late=True,
         )
 
     dhidden_two, branch_two, dcontext_two = branch(
@@ -1269,15 +1372,31 @@
                 [place, *index_out],
                 inputs,
                 scratch + [acc],
+                late=True,
             )
             blocks = outs[len(gain_outs) :]
             return outs[: len(gain_outs)], blocks[0::2], blocks[1::2]
         wholes = [low_shape(width, c) for c in columns]
         outs = run_kernel(
-            functools.partial(body, False), gain_outs + wholes, cost, [place], inputs, [acc]
+            functools.partial(body, False), gain_outs + wholes, cost, [place], inputs, [acc], late=True
         )
         return outs[: len(gain_outs)], *ring.halve_wholes(outs[len(gain_outs) :], block_rows)
 
+    patch_spans = [(side == 0, g) for side in range(2) for g in range(ring.groups)]
+    patch_shape = (ring.groups, own_patches, width)
+    memory_keep, memory_give = run_kernel(
+        functools.partial(rows_back_kernel, patch_spans, False),
+        [full_shape(*patch_shape), low_shape(*patch_shape)],
+        patches * width,
+        [],
+        [dkey, dvalue, heads_two],
+    )
+    memory_total = ring.pair_sum(memory_keep, memory_give)
+    part_g, memory_total = together(part_g, memory_total)
+    memory_sent = ring.group_terms(memory_total)
+    dhidden_one, branch_one, dcontext_one = branch(
+        1, hidden_one, part_low, part_g, out_one, out_one_g, [dhidden_two]
+    )
     (gain_two,), cross_keep, cross_give = grads(
         cross_grads_kernel,
         [
@@ -1291,27 +1410,17 @@
             dvalue,
             query_two,
             gain_cols,
+            context_one,
+            context_one_g,
+            branch_one,
         ],
-        (2 * half, 2 * half),
+        (3 * half, 2 * half),
         [full_shape(width, PAIR_LANES)],
         (both + patches) * width * half,
     )
-    patch_spans = [(side == 0, g) for side in range(2) for g in range(ring.groups)]
-    patch_shape = (ring.groups, own_patches, width)
-    memory_keep, memory_give = run_kernel(
-        functools.partial(rows_back_kernel, patch_spans, False),
-        [full_shape(*patch_shape), low_shape(*patch_shape)],
-        patches * width,
-        [],
-        [dkey, dvalue, key_two, value_two],
-    )
-    memory_total = ring.pair_sum(memory_keep, memory_give)
-    memory_sent = ring.group_terms(memory_total)
-    cross_got = ring.near_sends(cross_give, len(ring.tails[0]) - 1)
-
-    dhidden_one, branch_one, dcontext_one = branch(
-        1, hidden_one, part_low, part_g, out_one, out_one_g, [dhidden_two]
-    )
+    cross_got = ring.near_sends(cross_give, last)
+    cross_keep, dcontext_one = together(cross_keep, dcontext_one)
+
     dquery_one, dkey_one, dvalue_one = attention_backward(
         info_one,
         query_heads,
@@ -1323,58 +1432,34 @@
         True,
         token_chunk,
     )
-    dquery_one, dkey_one, dvalue_one, memory_sent, cross_got = together(
-        dquery_one, dkey_one, dvalue_one, memory_sent, cross_got
-    )
-    memory_grad = memory_sent
-    cross_left, cross_give = ring.near_sums(cross_keep, cross_got)
+    dquery_one, dkey_one, dvalue_one, cross_got, memory_grad = together(
+        dquery_one, dkey_one, dvalue_one, cross_got, memory_sent
+    )
+    for step in reversed(range(1, last + 1)):
+        cross_keep, cross_give = ring.near_sums(cross_keep, cross_got, step)
+        cross_got = ring.near_sends(cross_give, step - 1)
+    dquery_one, cross_give = together(dquery_one, cross_give)
     _, self_keep, self_give = grads(
         self_grads_kernel,
         [
-            context_one,
-            context_one_g,
-            branch_one,
             normed_one,
             dquery_one,
             dkey_one,
             dvalue_one,
             query_one,
-            key_one,
-            value_one,
+            heads_one,
             gain_cols,
             gain_two,
             gain_three,
         ],
-        (2 * half + PAIR_LANES, 2 * half),
+        (half + PAIR_LANES, 2 * half),
         [],
         (both + keys) * width * half,
     )
-    self_got = ring.near_sends(self_give, len(ring.tails[0]) - 1)
-    for step in range(len(ring.far)):
-        cross_left, cross_give = ring.far_sum(cross_left, cross_give, step)
-    cross_sum = cross_left[0]
-    self_left, self_give = ring.near_sums(self_keep, self_got)
-    late = self_give
-    for step in range(len(ring.far)):
-        if packed and step == len(ring.far) - 1:
-            self_give, mlp_sum = together(self_give, mlp_sum)
-        self_left, self_give = ring.far_sum(self_left, self_give, step)
-    if packed:
-        mlp_sum = mlp_sum.astype(F32)
-        take = lambda at, size: mlp_sum[:, at : at + size]
-        gate_up = jnp.concatenate(
-            [
-                jnp.concatenate([take((m * pieces + j) * hidden_half, hidden_half) for m in range(2)], axis=1)
-                for j in range(pieces)
-            ],
-            axis=0,
-        )
-        base = 2 * pieces * hidden_half
-        mlp_ddown = jnp.concatenate(
-            [take(base + j * width, width) for j in range(down_pieces)], axis=0
-        )
-
-    dquery_one, dkey_one, dvalue_one = after((dquery_one, dkey_one, dvalue_one), self_keep[0])
+    self_give, cross_got = together(self_give, cross_got)
+    self_got = ring.near_sends(self_give, last)
+    cross_own, cross_far = ring.far_first(cross_keep, cross_got)
+    dquery_one, dkey_one, dvalue_one = after((dquery_one, dkey_one, dvalue_one), self_give)
     token_spans = [(side == 0, g) for g in range(ring.groups) for side in range(2)]
     token_shape = (ring.groups, own, width)
     part_keep, part_give = run_kernel(
@@ -1382,26 +1467,48 @@
         [full_shape(*token_shape), low_shape(*token_shape)],
         keys * width,
         [],
-        [dkey_one, dvalue_one, key_one, value_one, dquery_one, query_one],
-    )
-    dnormed_one = ring.group_terms(after(ring.pair_sum(part_keep, part_give), late))
+        [dkey_one, dvalue_one, heads_one, dquery_one, query_one],
+    )
+    part_total = ring.pair_sum(part_keep, part_give)
+    self_got, cross_far, part_total = together(self_got, cross_far, part_total)
+    for step in reversed(range(1, last + 1)):
+        self_keep, self_give = ring.near_sums(self_keep, self_got, step)
+        self_got = ring.near_sends(self_give, step - 1)
+    cross_own, cross_far = ring.far_last(cross_own, cross_far)
+    self_got, cross_far, part_total = together(self_got, cross_far, part_total)
+    self_own, self_far = ring.far_sends(self_keep, self_got)
+    dnormed_one = ring.group_terms(part_total)
     plain, inverse = normalize(tokens[0].astype(F32))
     input_grad = dhidden_one[:own] + norm_back(plain, inverse, gain_rows[0:1], dnormed_one)
 
-    (gate_up,) = ring.finished(gate_up, 1)
-    gate_columns = [gate_up[:, i * hidden_half : (i + 1) * hidden_half] for i in range(4)]
-    mlp_dgate = unit_whole(gate_columns[0], gate_columns[2], units)
-    mlp_dup = unit_whole(gate_columns[1], gate_columns[3], units)
-    cross_dout, cross_dquery, cross_dkey, cross_dvalue = ring.finished(cross_sum, 4)
-    self_left, mlp_dgate, mlp_dup, mlp_ddown = together(self_left, mlp_dgate, mlp_dup, mlp_ddown)
-    self_sum = self_left[0]
-    gain_at = 2 * half
-    gain_block = self_sum[:, gain_at : gain_at + PAIR_LANES]
+    if packed:
+        mlp_rows = mlp_sum[:, : 2 * pieces * hidden_half].reshape(piece, 2, pieces, hidden_half)
+        mlp_rows = mlp_rows.transpose(2, 0, 1, 3).reshape(2 * rows, 2 * hidden_half)
+        mlp_give = lax.dynamic_slice_in_dim(mlp_rows, (1 - ring.half) * rows, rows, 0)
+        mlp_dgate, mlp_dup, mlp_ddown = run_kernel(
+            functools.partial(feed_forward_grads_kernel, pieces, units),
+            [full_shape(rows, 2 * hidden_half)] * 2 + [full_shape(units, width)],
+            rows * width,
+            [place],
+            [mlp_sum, ring.swap(mlp_give)],
+        )
+    else:
+        (gate_up,) = ring.finished(gate_up, 1)
+        gate_columns = [gate_up[:, i * hidden_half : (i + 1) * hidden_half] for i in range(4)]
+        mlp_dgate = unit_whole(gate_columns[0], gate_columns[2], units)
+        mlp_dup = unit_whole(gate_columns[1], gate_columns[3], units)
+    cross_sum = ring.far_sum(cross_own, cross_far)
+    cross_dout, cross_dquery, self_dout, cross_dkey, cross_dvalue = ring.finished(cross_sum, 5)
+    self_far, mlp_dgate, mlp_dup, mlp_ddown, input_grad, cross_dout = together(
+        self_far, mlp_dgate, mlp_dup, mlp_ddown, input_grad, cross_dout
+    )
+    self_sum = ring.far_sum(self_own, self_far)
+    gain_block = self_sum[:, half : half + PAIR_LANES]
     gain_block = jnp.pad(gain_block, ((0, 0), (0, half - PAIR_LANES)))
-    self_sum = jnp.concatenate(
-        [self_sum[:, :gain_at], self_sum[:, gain_at + PAIR_LANES :], gain_block], axis=1
-    )
-    self_dquery, self_dout, self_dkey, self_dvalue, gain_terms = ring.finished(self_sum, 5)
+    joined = jnp.concatenate(
+        [self_sum[:, :half], self_sum[:, half + PAIR_LANES :], gain_block], axis=1
+    )
+    self_dquery, self_dvalue, self_dkey, gain_terms = ring.finished(joined, 4)
     dgains = gain_terms[:, :3] + gain_terms[:, half : half + 3]
 
     return (

time: 368 us -> 360 us (0.978)
  starting transfers between devices: 63.2 us -> 42.1 us
  Pallas kernels: 140 us -> 150 us
  local copies, waits for them, and re-layouts: 24.3 us -> 14.8 us
  other arithmetic: 14.4 us -> 22.1 us
  waiting for transfers between devices: 105 us -> 109 us
    ppermute x25 -> x26, starting transfers between devices: 60.1 us -> 38.3 us  [send(): return lax.ppermute(values, axis, [(i, i ^ bit) for i in range(size)])]
    pallas_call x2, Pallas kernels: 25.6 us -> 33.7 us  [attention_backward(): pl.pallas_call(functools.partial(backward_kernel, causal, chunk, span), o...]
    ppermute x25 -> x26, waiting for transfers between devices: 94.3 us -> 100 us  [send(): return lax.ppermute(values, axis, [(i, i ^ bit) for i in range(size)])]
    add x4 -> x6, other arithmetic: 0.24 us -> 5.41 us  [the longest x1 2.27 us: on_device(): dhidden_one[:own] + norm_back(plain, inverse, gain_rows[0:1], dnormed_one)]
    pallas_call x2, Pallas kernels: 16.4 us -> 21.4 us  [attention_forward(): pl.pallas_call(functools.partial(forward_kernel, causal, chunk, span), ou...]
    unnamed x85 -> x72, local copies, waits for them, and re-layouts: 9.86 us -> 4.9 us
    reduce_scatter x1, waiting for transfers between devices: 4.97 us -> 0.02 us  [on_device(): lax.psum_scatter(mlp_terms, pairs, scatter_dimension=0, tiled=True)]
    pallas_call x18, Pallas kernels: 96.2 us -> 92.5 us  [run_kernel(): pl.pallas_call(functools.partial(staged_kernel, body, late, sizes), out_s...]
  transfers between devices with their start and end apart: 44 -> 45, of which waited for: 23 -> 24; matrix products, arithmetic and copies ran while one was open for 5% -> 8% of each run, Pallas kernels for 32% -> 36%
where the time goes in v1:
time: 360 us; the launch traced here: 354 us
  Pallas kernels  150 us (42%)
  waiting for transfers between devices  109 us (30%)
  starting transfers between devices  42.1 us (12%)
  other arithmetic  22.1 us (6%)
  between operations  16.4 us (5%)
  local copies, waits for them, and re-layouts  14.8 us (4%)
    ppermute x26, waiting for transfers between devices, send(): return lax.ppermute(values, axis, [(i, i ^ bit) for i in range(size)])  100 us
    pallas_call x18, Pallas kernels, run_kernel(): pl.pallas_call(functools.partial(staged_kernel, body, late, sizes), out_s...  92.5 us
    ppermute x26, starting transfers between devices, send(): return lax.ppermute(values, axis, [(i, i ^ bit) for i in range(size)])  38.3 us
    pallas_call x2, Pallas kernels, attention_backward(): pl.pallas_call(functools.partial(backward_kernel, causal, chunk, span), o...  33.7 us
    pallas_call x2, Pallas kernels, attention_forward(): pl.pallas_call(functools.partial(forward_kernel, causal, chunk, span), ou...  21.4 us
    ppermute x17, waiting for transfers between devices, swap(): return lax.ppermute(values, 'hc', [(0, 1), (1, 0)])  9.02 us
  transfers between devices with their start and end apart: 45, of which 24 were waited for; matrix products, arithmetic and copies ran while one was open for 8% of the time, Pallas kernels for 36%

profile of v1, /device:TPU:0, one launch (start us, length us, event | category | flops | bytes accessed | tf_op | source)
XLA Modules:
  0.0 354.4 jit_solution(8094845426937437842)
XLA Ops:
  23.5 6.4 %collective-permute-done.1 = bf16[1,48,2816]{2,1,0:T(8,128)(2,1)} collective-permute-done((bf16[1,48,2816]{2,1,0:T(8,128)(2,1)S(1)}, bf16[1,48,2816]{2,1,0:T(8,128)(2,1)}, u32[]{:S(2)}, u32[]{:S(2)}) %collective-permute-start.1) | collective-permute-done | bytes 270368 | tf_op jit(solution)/shard_map/ppermute | solution.py:922
  33.2 9.3 %collective-permute-done.4 = bf16[1,256,768]{2,1,0:T(8,128)(2,1)S(1)} collective-permute-done((bf16[1,256,768]{2,1,0:T(8,128)(2,1)S(1)}, bf16[1,256,768]{2,1,0:T(8,128)(2,1)S(1)}, u32[]{:S(2)}, u32[]{:S(2)}) %collective-permute-start.4) | collective-permute-done | bytes 393248 | tf_op jit(solution)/shard_map/ppermute | solution.py:922
  50.2 4.9 %collective-permute-done.8 = bf16[1,256,768]{2,1,0:T(8,128)(2,1)S(1)} collective-permute-done((bf16[1,256,768]{2,1,0:T(8,128)(2,1)S(1)}, bf16[1,256,768]{2,1,0:T(8,128)(2,1)S(1)}, u32[]{:S(2)}, u32[]{:S(2)}) %collective-permute-start.8) | collective-permute-done | bytes 393248 | tf_op jit(solution)/shard_map/ppermute | solution.py:922
  56.7 15.3 %collective-permute-done.6 = bf16[4,48,1536]{2,1,0:T(8,128)(2,1)S(1)} collective-permute-done((bf16[4,48,1536]{2,1,0:T(8,128)(2,1)S(1)}, bf16[4,48,1536]{2,1,0:T(8,128)(2,1)S(1)}, u32[]{:S(2)}, u32[]{:S(2)}) %collective-permute-start.6) | collective-permute-done | bytes 589856 | tf_op jit(solution)/shard_map/ppermute | solution.py:922
  78.9 8.3 %collective-permute-done.9.refs_3_ = bf16[8,48,512]{2,1,0:T(8,128)(2,1)} collective-permute-done((bf16[8,48,512]{2,1,0:T(8,128)(2,1)}, bf16[8,48,512]{2,1,0:T(8,128)(2,1)}, u32[]{:S(2)}, u32[]{:S(2)}) %collective-permute-start.9) | collective-permute-done | bytes 393248 | tf_op jit(solution)/shard_map/ppermute | solution.py:922
  93.4 6.2 %shard_map.333 = (f32[8,768]{1,0:T(8,128)}, bf16[1024,768]{1,0:T(8,128)(2,1)}, bf16[512,384]{1,0:T(8,128)(2,1)}, bf16[1024,384]{1,0:T(8,128)(2,1)}, bf16[1024,38...) custom-call(s32[16]{0:T(128)} %get-tuple-element.310.refs_0_, ...), custom_call_target="tpu_custom_call" | custom-call | flops 301989 | tf_op jit(solution)/shard_map/pallas_call | solution.py:346
  100.5 8.2 %shard_map.334 = (bf16[512,384]{1,0:T(8,128)(2,1)}, f32[3,2,512]{2,1,0:T(2,128)}) custom-call(s32[7]{0:T(128)} %pad_add_fusion.info, bf16[512,384]{1,0:T(8,128)(2,1)} %get-tuple-element.162.q_ref, bf16[1024,384]{1,0:T(8,128)(2,1)} %get-tuple-element.163.k_ref, bf16[1024,384]{1,0:T(8,128)(2,1)} %get-tuple-element.164.v_ref), custom_call_target="tpu_custom_call" | custom-call | flops 512 | tf_op jit(solution)/shard_map/pallas_call | solution.py:180
  108.7 9.2 %collective-permute-done.12.refs_2_ = bf16[8,48,768]{2,1,0:T(8,128)(2,1)} collective-permute-done((bf16[8,48,768]{2,1,0:T(8,128)(2,1)}, bf16[8,48,768]{2,1,0:T(8,128)(2,1)}, u32[]{:S(2)}, u32[]{:S(2)}) %collective-permute-start.12) | collective-permute-done | bytes 589856 | tf_op jit(solution)/shard_map/ppermute | solution.py:922
  124.8 7.3 %shard_map.335 = (bf16[2048,384]{1,0:T(8,128)(2,1)}, bf16[2048,384]{1,0:T(8,128)(2,1)}, bf16[768,768]{1,0:T(8,128)(2,1)}) custom-call(s32[16]{0:T(128)} %get-tuple-element.311.refs_1_.refs_0_, bf16[8,48,768]{2,1,0:T(8,128)(2,1)} %get-tuple-element.167.refs_1_, bf16[8,48,768]{2,1,0:T(8,128)(2,1)} %copy-done.23, bf16[1024,768]{1,0:T(8,128)(2,1)} %bitcast.46, ...), custom_call_target="tpu_custom_call" | custom-call | flops 603979 | tf_op jit(solution)/shard_map/pallas_call | solution.py:346
  133.1 4.6 %shard_map.337 = (f32[512,768]{1,0:T(8,128)}, bf16[512,768]{1,0:T(8,128)(2,1)}, bf16[512,384]{1,0:T(8,128)(2,1)}) custom-call(s32[1]{0:T(128)} %bitcast.refs_0_, bf16[256,768]{1,0:T(8,128)(2,1)} %slice_bitcast_fusion.1.refs_1_, bf16[256,768]{1,0:T(8,128)(2,1)} %slice_bitcast_fusion.refs_2_, bf16[512,384]{1,0:T(8,128)(2,1)} %get-tuple-element.169.refs_3_.refs_14_.c_ref, ...), custom_call_target="tpu_custom_call" | custom-call | flops 150994 | tf_op jit(solution)/shard_map/pallas_call | solution.py:346
  141.3 13.2 %shard_map.341 = (bf16[512,384]{1,0:T(8,128)(2,1)}, f32[3,2,512]{2,1,0:T(2,128)}) custom-call(s32[11]{0:T(128)} %pad_add_fusion.1.info, bf16[512,384]{1,0:T(8,128)(2,1)} %get-tuple-element.187.q_ref, bf16[2048,384]{1,0:T(8,128)(2,1)} %get-tuple-element.188.k_ref, bf16[2048,384]{1,0:T(8,128)(2,1)} %get-tuple-element.189.v_ref), custom_call_target="tpu_custom_call" | custom-call | flops 512 | tf_op jit(solution)/shard_map/pallas_call | solution.py:180
  157.5 15.3 %shard_map.342 = (f32[512,768]{1,0:T(8,128)}, bf16[512,768]{1,0:T(8,128)(2,1)}, f32[256,768]{1,0:T(8,128)}, bf16[256,768]{1,0:T(8,128)(2,1)}, f32[768,128]{1,0:T(8,128)}, /*index=5*/bf16[16,16,9216]{2,1,0:T(8,128)(2,1)}) custom-call(s32[1]{0:T(128)} %bitcast.refs_0_, f32[512,768]{1,0:T(8,128)} %get-tuple-element.178.refs_1_, ...), custom_call_target="tpu_custom_call" | custom-call | flops 805306 | tf_op jit(solution)/shard_map/pallas_call | solution.py:346
  176.3 4.9 %shard_map.343 = (f32[512,768]{1,0:T(8,128)}, bf16[512,768]{1,0:T(8,128)(2,1)}, bf16[512,384]{1,0:T(8,128)(2,1)}) custom-call(s32[1]{0:T(128)} %bitcast.refs_0_, f32[512,768]{1,0:T(8,128)} %get-tuple-element.194.refs_1_, f32[8,768]{1,0:T(8,128)} %get-tuple-element.176.refs_7_.refs_6_.refs_2_, bf16[512,768]{1,0:T(8,128)(2,1)} %get-tuple-element.198.refs_3_, ...), custom_call_target="tpu_custom_call" | custom-call | flops 150994 | tf_op jit(solution)/shard_map/pallas_call | solution.py:346
  181.2 21.4 %shard_map.344 = (bf16[512,384]{1,0:T(8,128)(2,1)}, bf16[2048,384]{1,0:T(8,128)(2,1)}, bf16[2048,384]{1,0:T(8,128)(2,1)}) custom-call(s32[11]{0:T(128)} %pad_add_fusion.1.info, bf16[512,384]{1,0:T(8,128)(2,1)} %get-tuple-element.187.q_ref, bf16[2048,384]{1,0:T(8,128)(2,1)} %get-tuple-element.188.k_ref, bf16[2048,384]{1,0:T(8,128)(2,1)} %get-tuple-element.189.v_ref, ...), custom_call_target="tpu_custom_call" | custom-call | flops 512 | tf_op jit(solution)/shard_map/pallas_call | solution.py:208
  202.6 6.9 %shard_map.346 = (f32[2,512,768]{2,1,0:T(8,128)}, bf16[2,512,768]{2,1,0:T(8,128)(2,1)}) custom-call(bf16[2048,384]{1,0:T(8,128)(2,1)} %get-tuple-element.204.refs_0_.refs_10_, bf16[2048,384]{1,0:T(8,128)(2,1)} %get-tuple-element.205.refs_1_.refs_11_, bf16[768,768]{1,0:T(8,128)(2,1)} %get-tuple-element.206.refs_2_), custom_call_target="tpu_custom_call" | custom-call | flops 1572 | tf_op jit(solution)/shard_map/pallas_call | solution.py:346
  218.0 5.1 %shard_map.347 = (f32[512,768]{1,0:T(8,128)}, bf16[512,768]{1,0:T(8,128)(2,1)}, bf16[512,384]{1,0:T(8,128)(2,1)}) custom-call(s32[1]{0:T(128)} %bitcast.refs_0_, f32[512,768]{1,0:T(8,128)} %get-tuple-element.178.refs_1_, f32[8,768]{1,0:T(8,128)} %get-tuple-element.176.refs_7_.refs_6_.refs_2_, bf16[512,768]{1,0:T(8,128)(2,1)} %shard_map.345.refs_3_, ...), custom_call_target="tpu_custom_call" | custom-call | flops 150994 | tf_op jit(solution)/shard_map/pallas_call | solution.py:346
  223.1 11.8 %shard_map.348 = (f32[768,128]{1,0:T(8,128)}, bf16[8,48,1152]{2,1,0:T(8,128)(2,1)}, bf16[8,48,1152]{2,1,0:T(8,128)(2,1)}, bf16[8,48,768]{2,1,0:T(8,128)(2,1)}, bf16[8,48,768]{2,1,0:T(8,128)(2,1)}) custom-call(s32[1]{0:T(128)} %bitcast.refs_0_, s32[16]{0:T(128)} %get-tuple-element.313.refs_1_, s32[16]{0:T(128)} %get-tuple-element.312.refs_2_, ...), custom_call_target="tpu_custom_call" | custom-call | flops 754974 | tf_op jit(solution)/shard_map/pallas_call | solution.py:346
  236.6 12.3 %shard_map.349 = (bf16[512,384]{1,0:T(8,128)(2,1)}, bf16[1024,384]{1,0:T(8,128)(2,1)}, bf16[1024,384]{1,0:T(8,128)(2,1)}) custom-call(s32[7]{0:T(128)} %pad_add_fusion.info, bf16[512,384]{1,0:T(8,128)(2,1)} %get-tuple-element.162.q_ref, bf16[1024,384]{1,0:T(8,128)(2,1)} %get-tuple-element.163.k_ref, bf16[1024,384]{1,0:T(8,128)(2,1)} %get-tuple-element.164.v_ref, ...), custom_call_target="tpu_custom_call" | custom-call | flops 512 | tf_op jit(solution)/shard_map/pallas_call | solution.py:208
  254.4 9.6 %collective-permute-done.24 = bf16[8,48,1152]{2,1,0:T(8,128)(2,1)S(1)} collective-permute-done((bf16[8,48,1152]{2,1,0:T(8,128)(2,1)}, bf16[8,48,1152]{2,1,0:T(8,128)(2,1)S(1)}, u32[]{:S(2)}, u32[]{:S(2)}) %collective-permute-start.24) | collective-permute-done | bytes 884768 | tf_op jit(solution)/shard_map/ppermute | solution.py:922
  267.1 7.4 %shard_map.350 = (bf16[8,48,512]{2,1,0:T(8,128)(2,1)}, bf16[8,48,512]{2,1,0:T(8,128)(2,1)}, bf16[8,48,768]{2,1,0:T(8,128)(2,1)}, bf16[8,48,768]{2,1,0:T(8,128)(2,1)}) custom-call(s32[1]{0:T(128)} %bitcast.refs_0_, s32[16]{0:T(128)} %get-tuple-element.313.refs_1_, s32[16]{0:T(128)} %get-tuple-element.312.refs_2_, ...), custom_call_target="tpu_custom_call" | custom-call | flops 452984 | tf_op jit(solution)/shard_map/pallas_call | solution.py:346
  279.3 5.7 %shard_map.351 = (f32[2,256,768]{2,1,0:T(8,128)}, bf16[2,256,768]{2,1,0:T(8,128)(2,1)}) custom-call(bf16[1024,384]{1,0:T(8,128)(2,1)} %get-tuple-element.242.refs_5_.refs_0_, bf16[1024,384]{1,0:T(8,128)(2,1)} %get-tuple-element.243.refs_6_.refs_1_, bf16[768,768]{1,0:T(8,128)(2,1)} %get-tuple-element.232.refs_8_.refs_2_, ...), custom_call_target="tpu_custom_call" | custom-call | flops 786 | tf_op jit(solution)/shard_map/pallas_call | solution.py:346
  287.9 11.6 %collective-permute-done.31 = bf16[2,48,1920]{2,1,0:T(8,128)(2,1)S(1)} collective-permute-done((bf16[2,48,1920]{2,1,0:T(8,128)(2,1)S(1)}, bf16[2,48,1920]{2,1,0:T(8,128)(2,1)S(1)}, u32[]{:S(2)}, u32[]{:S(2)}) %collective-permute-start.31) | collective-permute-done | bytes 368672 | tf_op jit(solution)/shard_map/ppermute | solution.py:922
  301.9 5.1 %collective-permute-start.35 = (bf16[1,48,1920]{2,1,0:T(8,128)(2,1)}, bf16[1,48,1920]{2,1,0:T(8,128)(2,1)}, u32[]{:S(2)}, u32[]{:S(2)}) collective-permute-start(bf16[1,48,1920]{2,1,0:T(8,128)(2,1)} %fusion.10), channel_id=1, source_target_pairs={{0,16},{4,20},{8,24},{12,28},{16,0},{20,4},{24,8},{28,12},{1,17},{... | collective-permute-start | bytes 552968 | tf_op jit(solution)/shard_map/ppermute | solution.py:922
  310.4 6.2 %collective-permute-done.35 = bf16[1,48,1920]{2,1,0:T(8,128)(2,1)} collective-permute-done((bf16[1,48,1920]{2,1,0:T(8,128)(2,1)}, bf16[1,48,1920]{2,1,0:T(8,128)(2,1)}, u32[]{:S(2)}, u32[]{:S(2)}) %collective-permute-start.35) | collective-permute-done | bytes 184352 | tf_op jit(solution)/shard_map/ppermute | solution.py:922
  (239 shorter events, 121.6 us)
Async XLA Ops:
  7.2 130.5 %all-gather.2.cloned.1.call-start = ((), (), s32[]{:S(2)}) async-start(), calls=%async_computation.1 | async-start | bytes 5640192 | tf_op jit(solution)/shard_map/all_gather | solution.py:1146
  10.9 12.5 %collective-permute-start.2 = (bf16[1,256,768]{2,1,0:T(8,128)(2,1)}, bf16[1,256,768]{2,1,0:T(8,128)(2,1)S(1)}, u32[]{:S(2)}, u32[]{:S(2)}) collective-permute-start(bf16[1,256,768]{2,1,0:T(8,128)(2,1)} %param.21), channel_id=1, source_target_pairs={{0,2},{2,0},{1,3},{3,1},{4,6},{6,4},{5,7},{7,5},{8,10},{10,8},{9,1... | collective-permute-start | bytes 1179656 | tf_op jit(solution)/shard_map/ppermute | solution.py:922
  14.5 15.4 %collective-permute-start.1 = (bf16[1,48,2816]{2,1,0:T(8,128)(2,1)S(1)}, bf16[1,48,2816]{2,1,0:T(8,128)(2,1)}, u32[]{:S(2)}, u32[]{:S(2)}) collective-permute-start(bf16[1,48,2816]{2,1,0:T(8,128)(2,1)S(1)} %maximum_bitcast_fusion), channel_id=1, source_target_pairs={{0,16},{4,20},{8,24},{12,28},{16,0},{20,4},{24,8},{28,12},{1,17},{... | collective-permute-start | bytes 811016 | tf_op jit(solution)/shard_map/ppermute | solution.py:922
  30.9 302.4 %reduce-scatter.2.cloned.1.call-start = ((), (), s32[]{:S(2)}) async-start(), calls=%async_computation.2 | async-start | bytes 5013504 | tf_op jit(solution)/shard_map/reduce_scatter | solution.py:1299
  30.9 16.0 %collective-permute-start.3 = (bf16[2,48,2816]{2,1,0:T(8,128)(2,1)S(1)}, bf16[2,48,2816]{2,1,0:T(8,128)(2,1)S(1)}, u32[]{:S(2)}, u32[]{:S(2)}) collective-permute-start(bf16[2,48,2816]{2,1,0:T(8,128)(2,1)S(1)} %pad_maximum_fusion.6), channel_id=1, source_target_pairs={{0,8},{4,12},{8,0},{12,4},{16,24},{20,28},{24,16},{28,20},{1,9},{5... | collective-permute-start | bytes 1622024 | tf_op jit(solution)/shard_map/ppermute | solution.py:922
  48.7 23.3 %collective-permute-start.6 = (bf16[4,48,1536]{2,1,0:T(8,128)(2,1)S(1)}, bf16[4,48,1536]{2,1,0:T(8,128)(2,1)S(1)}, u32[]{:S(2)}, u32[]{:S(2)}) collective-permute-start(bf16[4,48,1536]{2,1,0:T(8,128)(2,1)S(1)} %slice.215), channel_id=1, source_target_pairs={{0,2},{2,0},{1,3},{3,1},{4,6},{6,4},{5,7},{7,5},{8,10},{10,8},{9,1... | collective-permute-start | bytes 1769480 | tf_op jit(solution)/shard_map/ppermute | solution.py:922
  50.2 21.9 %collective-permute-start.7 = (bf16[2,256,768]{2,1,0:T(8,128)(2,1)S(1)}, bf16[2,256,768]{2,1,0:T(8,128)(2,1)S(1)}, u32[]{:S(2)}, u32[]{:S(2)}) collective-permute-start(bf16[2,256,768]{2,1,0:T(8,128)(2,1)S(1)} %pad_maximum_fusion.3.refs_6_), channel_id=1, source_target_pairs={{0,1},{1,0},{2,3},{3,2},{4,5},{5,4},{6,7},{7,6},{8,9},{9,8},{10,11... | collective-permute-start | bytes 2359304 | tf_op jit(solution)/shard_map/ppermute | solution.py:925
  72.2 17.2 %collective-permute-start.11 = (bf16[2,512,768]{2,1,0:T(8,128)(2,1)S(1)}, bf16[2,512,768]{2,1,0:T(8,128)(2,1)S(1)}, u32[]{:S(2)}, u32[]{:S(2)}) collective-permute-start(bf16[2,512,768]{2,1,0:T(8,128)(2,1)S(1)} %constant_dynamic-update-slice_fusion), channel_id=1, source_target_pairs={{0,1},{1,0},{2,3},{3,2},{4,5},{5,4},{6,7},{7,6},{8,9},{9,8},{10,11... | collective-permute-start | bytes 4718600 | tf_op jit(solution)/shard_map/ppermute | solution.py:925
  73.5 15.9 %collective-permute-start.10 = (bf16[8,48,768]{2,1,0:T(8,128)(2,1)}, bf16[8,48,768]{2,1,0:T(8,128)(2,1)}, u32[]{:S(2)}, u32[]{:S(2)}) collective-permute-start(bf16[8,48,768]{2,1,0:T(8,128)(2,1)} %get-tuple-element.289.refs_4_), channel_id=1, source_target_pairs={{0,4},{4,0},{8,12},{12,8},{16,20},{20,16},{24,28},{28,24},{1,5},{5... | collective-permute-start | bytes 1769480 | tf_op jit(solution)/shard_map/ppermute | solution.py:922
  89.4 28.5 %collective-permute-start.12 = (bf16[8,48,768]{2,1,0:T(8,128)(2,1)}, bf16[8,48,768]{2,1,0:T(8,128)(2,1)}, u32[]{:S(2)}, u32[]{:S(2)}) collective-permute-start(bf16[8,48,768]{2,1,0:T(8,128)(2,1)} %slice.220.refs_1_), channel_id=1, source_target_pairs={{0,2},{2,0},{1,3},{3,1},{4,6},{6,4},{5,7},{7,5},{8,10},{10,8},{9,1... | collective-permute-start | bytes 1769480 | tf_op jit(solution)/shard_map/ppermute | solution.py:922
  91.0 28.4 %collective-permute-start.13 = (bf16[8,48,768]{2,1,0:T(8,128)(2,1)}, bf16[8,48,768]{2,1,0:T(8,128)(2,1)S(1)}, u32[]{:S(2)}, u32[]{:S(2)}) collective-permute-start(bf16[8,48,768]{2,1,0:T(8,128)(2,1)} %get-tuple-element.167.refs_1_), channel_id=1, source_target_pairs={{0,4},{4,0},{8,12},{12,8},{16,20},{20,16},{24,28},{28,24},{1,5},{5... | collective-permute-start | bytes 1769480 | tf_op jit(solution)/shard_map/ppermute | solution.py:922
  139.8 16.7 %collective-permute-start.19 = (bf16[768,384]{1,0:T(8,128)(2,1)}, bf16[768,384]{1,0:T(8,128)(2,1)S(1)}, u32[]{:S(2)}, u32[]{:S(2)}) collective-permute-start(bf16[768,384]{1,0:T(8,128)(2,1)} %shard_map.340.refs_4_.refs_5_), channel_id=1, source_target_pairs={{0,1},{1,0},{2,3},{3,2},{4,5},{5,4},{6,7},{7,6},{8,9},{9,8},{10,11... | collective-permute-start | bytes 1769480 | tf_op jit(solution)/shard_map/ppermute | solution.py:925
  215.6 33.4 %collective-permute-start.26 = (bf16[1,512,768]{2,1,0:T(8,128)(2,1)S(1)}, bf16[1,512,768]{2,1,0:T(8,128)(2,1)S(1)}, u32[]{:S(2)}, u32[]{:S(2)}) collective-permute-start(bf16[1,512,768]{2,1,0:T(8,128)(2,1)S(1)} %slice.377), channel_id=1, source_target_pairs={{0,2},{2,0},{1,3},{3,1},{4,6},{6,4},{5,7},{7,5},{8,10},{10,8},{9,1... | collective-permute-start | bytes 2359304 | tf_op jit(solution)/shard_map/ppermute | solution.py:922
  235.0 29.0 %collective-permute-start.24 = (bf16[8,48,1152]{2,1,0:T(8,128)(2,1)}, bf16[8,48,1152]{2,1,0:T(8,128)(2,1)S(1)}, u32[]{:S(2)}, u32[]{:S(2)}) collective-permute-start(bf16[8,48,1152]{2,1,0:T(8,128)(2,1)} %get-tuple-element.220), channel_id=1, source_target_pairs={{0,2},{2,0},{1,3},{3,1},{4,6},{6,4},{5,7},{7,5},{8,10},{10,8},{9,1... | collective-permute-start | bytes 2654216 | tf_op jit(solution)/shard_map/ppermute | solution.py:922
  235.6 18.8 %collective-permute-start.25 = (bf16[8,48,768]{2,1,0:T(8,128)(2,1)}, bf16[8,48,768]{2,1,0:T(8,128)(2,1)S(1)}, u32[]{:S(2)}, u32[]{:S(2)}) collective-permute-start(bf16[8,48,768]{2,1,0:T(8,128)(2,1)} %get-tuple-element.221), channel_id=1, source_target_pairs={{0,4},{4,0},{8,12},{12,8},{16,20},{20,16},{24,28},{28,24},{1,5},{5... | collective-permute-start | bytes 1769480 | tf_op jit(solution)/shard_map/ppermute | solution.py:922
  264.2 12.6 %collective-permute-start.27 = (bf16[4,48,1152]{2,1,0:T(8,128)(2,1)S(1)}, bf16[4,48,1152]{2,1,0:T(8,128)(2,1)S(1)}, u32[]{:S(2)}, u32[]{:S(2)}) collective-permute-start(bf16[4,48,1152]{2,1,0:T(8,128)(2,1)S(1)} %get-tuple-element.283), channel_id=1, source_target_pairs={{0,4},{4,0},{8,12},{12,8},{16,20},{20,16},{24,28},{28,24},{1,5},{5... | collective-permute-start | bytes 1327112 | tf_op jit(solution)/shard_map/ppermute | solution.py:922
  276.8 22.7 %collective-permute-start.29 = (bf16[8,48,512]{2,1,0:T(8,128)(2,1)}, bf16[8,48,512]{2,1,0:T(8,128)(2,1)S(1)}, u32[]{:S(2)}, u32[]{:S(2)}) collective-permute-start(bf16[8,48,512]{2,1,0:T(8,128)(2,1)} %get-tuple-element.238), channel_id=1, source_target_pairs={{0,2},{2,0},{1,3},{3,1},{4,6},{6,4},{5,7},{7,5},{8,10},{10,8},{9,1... | collective-permute-start | bytes 1179656 | tf_op jit(solution)/shard_map/ppermute | solution.py:922
  278.3 22.9 %collective-permute-start.30 = (bf16[8,48,768]{2,1,0:T(8,128)(2,1)}, bf16[8,48,768]{2,1,0:T(8,128)(2,1)S(1)}, u32[]{:S(2)}, u32[]{:S(2)}) collective-permute-start(bf16[8,48,768]{2,1,0:T(8,128)(2,1)} %get-tuple-element.239), channel_id=1, source_target_pairs={{0,4},{4,0},{8,12},{12,8},{16,20},{20,16},{24,28},{28,24},{1,5},{5... | collective-permute-start | bytes 1769480 | tf_op jit(solution)/shard_map/ppermute | solution.py:922
  285.4 14.1 %collective-permute-start.31 = (bf16[2,48,1920]{2,1,0:T(8,128)(2,1)S(1)}, bf16[2,48,1920]{2,1,0:T(8,128)(2,1)S(1)}, u32[]{:S(2)}, u32[]{:S(2)}) collective-permute-start(bf16[2,48,1920]{2,1,0:T(8,128)(2,1)S(1)} %pad_maximum_fusion.8), channel_id=1, source_target_pairs={{0,8},{4,12},{8,0},{12,4},{16,24},{20,28},{24,16},{28,20},{1,9},{5... | collective-permute-start | bytes 1105928 | tf_op jit(solution)/shard_map/ppermute | solution.py:922
  301.9 14.6 %collective-permute-start.35 = (bf16[1,48,1920]{2,1,0:T(8,128)(2,1)}, bf16[1,48,1920]{2,1,0:T(8,128)(2,1)}, u32[]{:S(2)}, u32[]{:S(2)}) collective-permute-start(bf16[1,48,1920]{2,1,0:T(8,128)(2,1)} %fusion.10), channel_id=1, source_target_pairs={{0,16},{4,20},{8,24},{12,28},{16,0},{20,4},{24,8},{28,12},{1,17},{... | collective-permute-start | bytes 552968 | tf_op jit(solution)/shard_map/ppermute | solution.py:922
  310.3 31.3 %collective-permute-start.20 = (bf16[256,768]{1,0:T(8,128)(2,1)}, bf16[256,768]{1,0:T(8,128)(2,1)}, u32[]{:S(2)}, u32[]{:S(2)}) collective-permute-start(bf16[256,768]{1,0:T(8,128)(2,1)} %get-tuple-element.196), channel_id=1, source_target_pairs={{0,1},{1,0},{2,3},{3,2},{4,5},{5,4},{6,7},{7,6},{8,9},{9,8},{10,11... | collective-permute-start | bytes 1179656 | tf_op jit(solution)/shard_map/ppermute | solution.py:925
  319.2 20.7 %collective-permute-start.36 = (bf16[1,48,1280]{2,1,0:T(8,128)(2,1)}, bf16[1,48,1280]{2,1,0:T(8,128)(2,1)S(1)}, u32[]{:S(2)}, u32[]{:S(2)}) collective-permute-start(bf16[1,48,1280]{2,1,0:T(8,128)(2,1)} %pad_maximum_fusion.9), channel_id=1, source_target_pairs={{0,16},{4,20},{8,24},{12,28},{16,0},{20,4},{24,8},{28,12},{1,17},{... | collective-permute-start | bytes 368648 | tf_op jit(solution)/shard_map/ppermute | solution.py:922
  319.9 20.0 %collective-permute-start.37 = (bf16[1,48,1280]{2,1,0:T(8,128)(2,1)}, bf16[1,48,1280]{2,1,0:T(8,128)(2,1)}, u32[]{:S(2)}, u32[]{:S(2)}) collective-permute-start(bf16[1,48,1280]{2,1,0:T(8,128)(2,1)} %pad_maximum_fusion.10), channel_id=1, source_target_pairs={{0,8},{4,12},{8,0},{12,4},{16,24},{20,28},{24,16},{28,20},{1,9},{5... | collective-permute-start | bytes 368648 | tf_op jit(solution)/shard_map/ppermute | solution.py:922
  325.5 14.4 %collective-permute-start.38 = (bf16[1,48,1280]{2,1,0:T(8,128)(2,1)S(1)}, bf16[1,48,1280]{2,1,0:T(8,128)(2,1)S(1)}, u32[]{:S(2)}, u32[]{:S(2)}) collective-permute-start(bf16[1,48,1280]{2,1,0:T(8,128)(2,1)S(1)} %pad_maximum_fusion.11), channel_id=1, source_target_pairs={{0,24},{4,28},{8,16},{12,20},{16,8},{20,12},{24,0},{28,4},{1,25},{... | collective-permute-start | bytes 368648 | tf_op jit(solution)/shard_map/ppermute | solution.py:922
  (56 other events, 424.0 us)
Sparse Core Ops, SparseCore 0:
  31.0 105.6 all-gather.1
  173.4 158.1 reduce-scatter.1
